TPU v7x, 32 devices: a whole 2x2x4 slice. The times are simulated.
32 devices in a mesh: ta: 2 (over core), ha: 2 (over x), wa: 8 (over z, y).
Axes of the slice: x: 2, y: 2, z: 4, core: 2. Of those that a mesh axis runs over, the one named last changes fastest.
Arguments:
- features: bfloat16 [2, 16, 28, 112, 1024], P(None, 'ta', 'ha', 'wa'), may hold values from -6 to 6
- teacher: bfloat16 [2, 16, 28, 112, 1000], P(None, 'ta', 'ha', 'wa'), may hold values from -30 to 750
- head_weight: float32 [1024, 1000], replicated, may hold values from -0.1875 to 0.1875
Outputs:
- feature_grad: bfloat16 [2, 16, 28, 112, 1024], P(None, 'ta', 'ha', 'wa')
- loss: float32 [], replicated
- new_weight: float32 [1024, 1000], P(('ta', 'ha', 'wa'))
All inputs are finite; a program needn't handle non-finite values.
Results may differ from a plain program's by a relative error of at most 0.0056.
Values may be sent and summed in bfloat16 or wider, within the bound.
A program may use at most 192 MiB of HBM per device.

v0:
```python
import jax
import jax.numpy as jnp
from jax import lax
from jax.sharding import PartitionSpec as P

WW = 14
WV = 28


sharpness_divisor = 2.0
learn_rate = 0.1
clip_norm = 1000.0


def with_halo(block, sides, width):
    for axis, dim in sides:
        count = lax.axis_size(axis)
        forward = [(i, i + 1) for i in range(count - 1)]
        backward = [(target, source) for source, target in forward]
        low = lax.ppermute(
            lax.slice_in_dim(block, block.shape[dim] - width, None, axis=dim), axis, forward
        )
        high = lax.ppermute(lax.slice_in_dim(block, 0, width, axis=dim), axis, backward)
        block = jnp.concatenate([low, block, high], axis=dim)
    return block


def three_sum(padded, reduce_dimension, length):
    first = lax.slice_in_dim(padded, 0, length, axis=reduce_dimension)
    middle = lax.slice_in_dim(padded, 1, length + 1, axis=reduce_dimension)
    last = lax.slice_in_dim(padded, 2, length + 2, axis=reduce_dimension)
    return first + middle + last


def edge_count(position, length):
    return 3.0 - (position == 0).astype(jnp.float32) - (position == length - 1).astype(jnp.float32)


def clip_of(columns):
    return (columns + WV - WW // 2) // WV


def local(features, teacher, head_weight):
    batch, frames, rows, columns, width = features.shape
    classes = teacher.shape[-1]
    grid_wide = columns * lax.axis_size("wa")
    time_index = lax.axis_index("ta")
    height_index = lax.axis_index("ha")
    width_index = lax.axis_index("wa")
    frame_pos = time_index * frames + jnp.arange(frames, dtype=jnp.int32)
    row_pos = height_index * rows + jnp.arange(rows, dtype=jnp.int32)
    column_pos = width_index * columns + jnp.arange(columns, dtype=jnp.int32)
    own_clip = clip_of(column_pos)
    left_ok = (
        ((column_pos > 0) & (clip_of(column_pos - 1) == own_clip))
        .astype(jnp.float32)
        .reshape(1, 1, 1, columns, 1)
    )
    right_ok = (
        ((column_pos < grid_wide - 1) & (clip_of(column_pos + 1) == own_clip))
        .astype(jnp.float32)
        .reshape(1, 1, 1, columns, 1)
    )
    counts = (
        edge_count(frame_pos, frames * lax.axis_size("ta")).reshape(1, frames, 1, 1, 1)
        * edge_count(row_pos, rows * lax.axis_size("ha")).reshape(1, 1, rows, 1, 1)
        * (1.0 + left_ok + right_ok)
    )
    padded = with_halo(teacher, (("ta", 1), ("ha", 2), ("wa", 3)), 1)
    summed = three_sum(padded.astype(jnp.float32), 1, frames)
    summed = three_sum(summed, 2, rows)
    summed = (
        summed[:, :, :, 0:columns] * left_ok
        + summed[:, :, :, 1 : columns + 1]
        + summed[:, :, :, 2 : columns + 2] * right_ok
    )
    averaged_scores = (summed / counts).reshape(-1, classes)
    head_bf = head_weight.astype(jnp.bfloat16)
    feat_rows = features.reshape(-1, width)
    pupil_scores = jnp.dot(feat_rows, head_bf, preferred_element_type=jnp.float32)
    pupil_entropy_terms = jax.nn.log_softmax(pupil_scores / sharpness_divisor, axis=-1)
    mentor_entropy_terms = jax.nn.log_softmax(averaged_scores / sharpness_divisor, axis=-1)
    mentor_likelihoods = jnp.exp(mentor_entropy_terms)
    pupil_likelihoods = jnp.exp(pupil_entropy_terms)
    patch_kullback_leibler = jnp.sum(
        mentor_likelihoods * (mentor_entropy_terms - pupil_entropy_terms), axis=-1
    )
    piece_objective = sharpness_divisor * sharpness_divisor * jnp.sum(patch_kullback_leibler)
    score_slope = (sharpness_divisor * (pupil_likelihoods - mentor_likelihoods)).astype(
        jnp.bfloat16
    )
    feat_grad = lax.dot_general(
        score_slope, head_bf, (((1,), (1,)), ((), ())), preferred_element_type=jnp.float32
    )
    feature_grad = feat_grad.astype(jnp.bfloat16).reshape(features.shape)
    owned = width // lax.axis_size(("ta", "ha", "wa"))
    first_row = lax.axis_index(("ta", "ha", "wa")) * owned
    local_grad = lax.dot_general(
        feat_rows, score_slope, (((0,), (0,)), ((), ())), preferred_element_type=jnp.float32
    )
    head_grad, loss = lax.psum((local_grad, piece_objective), ("ta", "ha", "wa"))
    squares = jnp.sum(head_grad * head_grad)
    mine = lax.dynamic_slice_in_dim(head_grad, first_row, owned, 0)
    grad_norm = jnp.sqrt(squares)
    clip = jnp.minimum(1.0, clip_norm / (grad_norm + 1e-06))
    weight_rows = lax.dynamic_slice_in_dim(head_weight, first_row, owned, 0)
    new_weight = weight_rows - learn_rate * clip * mine
    return (feature_grad, loss, new_weight)


def solution(mesh):
    placed = (P(None, "ta", "ha", "wa", None), P(None, "ta", "ha", "wa", None), P())
    return jax.shard_map(
        local,
        mesh=mesh,
        in_specs=placed,
        out_specs=(P(None, "ta", "ha", "wa", None), P(), P(("ta", "ha", "wa"), None)),
        check_vma=False,
    )
```

profile of v0, /device:TPU:0, one launch (start us, length us, event | category | flops | bytes accessed | tf_op | source)
XLA Modules:
  0.0 394.2 jit_solution(16965063830056994423)
XLA Ops:
  7.2 0.0 all-reduce.2.cloned.1.call-start
  7.2 0.0 copy-start.2
  7.2 8.3 %fusion.11 = (bf16[2,1,14,14,1000]{4,1,3,2,0:T(2,128)(2,1)S(1)}, bf16[2,1,14,14,1000]{4,1,3,2,0:T(2,128)(2,1)S(1)}) fusion(bf16[2,8,14,14,1000]{4,1,3,2,0:T(8,128)(2,1)} %param.5), kind=kLoop, calls=%fused_computation.51 | loop fusion | bytes 3136000 | tf_op jit(solution)/shard_map/slice | solution.py:23
  15.5 1.3 copy.26
  16.8 2.4 collective-permute-start
  19.2 1.2 copy.27
  20.4 1.3 collective-permute-start.1
  21.7 0.0 copy-done.2
  21.7 6.7 %copy.14 = bf16[2,8,14,14,1024]{4,3,2,1,0:T(8,128)(2,1)} copy(bf16[2,8,14,14,1024]{4,1,3,2,0:T(8,128)(2,1)S(1)} %copy-done.2) | data formatting | bytes 12845056 | tf_op args[0]
  28.4 10.1 %reshape.134 = bf16[3136,1024]{1,0:T(8,128)(2,1)} reshape(bf16[2,8,14,14,1024]{4,3,2,1,0:T(8,128)(2,1)} %copy.14) | data formatting | bytes 12845056 | tf_op jit(solution)/shard_map/reshape | solution.py:79
  38.6 11.1 %multiply_reduce_fusion.1 = (f32[3136]{0:T(1024)S(1)}, f32[3136,1000]{0,1:T(8,128)S(1)}) fusion(bf16[3136,1024]{1,0:T(8,128)(2,1)} %reshape.134, f32[1024,1000]{0,1:T(8,128)} %param.6), kind=kOutput, calls=%fused_computation.15 | convolution fusion | flops 6429820928 | bytes 23075072 | tf_op jit(solution)/shard_map/dot_general | solution.py:80
  49.7 0.0 copy-start.1
  49.7 0.0 collective-permute-done
  49.7 1.1 constant_dynamic-update-slice_fusion.2
  50.8 13.1 %constant_dynamic-update-slice_fusion.1 = bf16[2,10,14,14,1000]{4,3,2,1,0:T(8,128)(2,1)} fusion(bf16[2,10,14,14,1000]{4,3,2,1,0:T(8,128)(2,1)} %constant_dynamic-update-slice_fusion.2, bf16[2,8,14,14,1000]{4,1,3,2,0:T(8,128)(2,1)} %param.5), kind=kLoop, calls=%fused_computation.30 | loop fusion | bytes 13762560
  63.9 0.0 collective-permute-done.1
  63.9 1.1 constant_dynamic-update-slice_fusion
  65.0 2.5 fusion.10
  67.5 4.2 %collective-permute-start.2 = (bf16[2,10,1,14,1000]{4,3,2,1,0:T(8,128)(2,1)}, bf16[2,10,1,14,1000]{4,3,2,1,0:T(8,128)(2,1)S(1)}, u32[]{:S(2)}, u32[]{:S(2)}) collective-permute-start(bf16[2,10,1,14,1000]{4,3,2,1,0:T(8,128)(2,1)} %get-tuple-element.17), channel_id=1, source_target_pairs={{0,8},{1,9},{2,10},{3,11},{4,12},{5,13},{6,14},{7,15},{16,24},{17,... | collective-permute-start | bytes 1680008 | tf_op jit(solution)/shard_map/ppermute | solution.py:20
  71.7 1.3 collective-permute-start.3
  73.0 2.1 exponential_reduce_fusion.1
  75.2 0.0 copy-done.1
  75.2 0.0 slice-start
  75.2 0.0 slice-start.1
  75.2 11.7 %collective-permute-done.2 = bf16[2,10,1,14,1000]{4,3,2,1,0:T(8,128)(2,1)S(1)} collective-permute-done((bf16[2,10,1,14,1000]{4,3,2,1,0:T(8,128)(2,1)}, bf16[2,10,1,14,1000]{4,3,2,1,0:T(8,128)(2,1)S(1)}, u32[]{:S(2)}, u32[]{:S(2)}) %collective-permute-start.2) | collective-permute-done | bytes 560032 | tf_op jit(solution)/shard_map/ppermute | solution.py:20
  86.9 4.5 %collective-permute-done.3 = bf16[2,10,1,14,1000]{4,3,2,1,0:T(8,128)(2,1)S(1)} collective-permute-done((bf16[2,10,1,14,1000]{4,3,2,1,0:T(8,128)(2,1)}, bf16[2,10,1,14,1000]{4,3,2,1,0:T(8,128)(2,1)S(1)}, u32[]{:S(2)}, u32[]{:S(2)}) %collective-permute-start.3) | collective-permute-done | bytes 560032 | tf_op jit(solution)/shard_map/ppermute | solution.py:23
  91.4 6.0 %pad_maximum_fusion.2 = (bf16[2,10,16,1,1000]{4,3,2,1,0:T(2,128)(2,1)S(1)}, bf16[2,10,16,1,1000]{4,3,2,1,0:T(2,128)(2,1)S(1)}) fusion(bf16[2,10,1,14,1000]{4,3,2,1,0:T(8,128)(2,1)S(1)} %collective-permute-done.3, bf16[2,10,14,14,1000]{4,3,2,1,0:T(8,128)(2,1)} %constant_dynamic-update-slice_fusion, bf16[2,10,1,14,1000]{4,3,2,1,0:T(8,128)(2,1)S(1)} %collective-permute-done.2), kind=kLoop, calls=%fused_computation.23 | loop fusion | flops 3840000 | bytes 10240000 | tf_op jit(solution)/shard_map/slice | solution.py:21
  97.4 0.0 slice-start.2
  97.4 0.2 copy.18
  97.6 3.5 collective-permute-start.4
  101.1 0.2 copy.19
  101.3 1.3 collective-permute-start.5
  102.6 0.1 broadcast_multiply_fusion.1
  102.7 0.1 broadcast_multiply_fusion
  102.8 26.4 %collective-permute-done.4 = bf16[2,10,16,1,1000]{4,2,3,1,0:T(8,128)(2,1)S(1)} collective-permute-done((bf16[2,10,16,1,1000]{4,2,3,1,0:T(8,128)(2,1)S(1)}, bf16[2,10,16,1,1000]{4,2,3,1,0:T(8,128)(2,1)S(1)}, u32[]{:S(2)}, u32[]{:S(2)}) %collective-permute-start.4) | collective-permute-done | bytes 640032 | tf_op jit(solution)/shard_map/ppermute | solution.py:20
  129.2 1.2 copy.20
  130.5 0.0 collective-permute-done.5
  130.5 1.2 copy.21
  131.7 0.0 slice-done
  131.7 0.0 slice-done.1
  131.7 0.0 slice-done.2
  131.7 7.9 %maximum_convert_fusion = f32[2,10,16,16,1000]{4,3,2,1,0:T(8,128)S(1)} fusion(bf16[2,10,16,1,1000]{4,3,2,1,0:T(2,128)(2,1)S(1)} %copy.21, bf16[2,10,1,14,1000]{4,3,2,1,0:T(8,128)(2,1)S(1)} %collective-permute-done.3, bf16[2,10,14,14,1000]{4,3,2,1,0:T(8,128)(2,1)S(1)} %bitcast.7, bf16[2,10,1,14,1000]{4,3,2,1,0:T(8,128)(2,1)S(1)} %collective-permute-done.2, ...), kind=kLoop, calls=%fused_computation.17 | loop fusion | flops 51200000 | bytes 30720000 | tf_op jit(solution)/shard_map/convert_element_type | solution.py:70
  139.7 9.0 %slice_add_fusion = f32[2,8,16,16,1000]{4,3,2,1,0:T(8,128)} fusion(f32[2,10,16,16,1000]{4,3,2,1,0:T(8,128)S(1)} %maximum_convert_fusion), kind=kLoop, calls=%fused_computation | loop fusion | flops 8192000 | bytes 65536000 | tf_op jit(solution)/shard_map/add | solution.py:32
  148.6 15.5 %slice_add_fusion.3 = f32[2,8,14,16,1000]{4,3,2,1,0:T(8,128)S(1)} fusion(f32[2,8,16,16,1000]{4,3,2,1,0:T(8,128)} %slice_add_fusion), kind=kLoop, calls=%fused_computation.8 | loop fusion | flops 7168000 | bytes 57344000 | tf_op jit(solution)/shard_map/add | solution.py:32
  164.2 9.3 %fusion.2 = f32[2,8,14,14,1000]{4,3,2,1,0:T(8,128)} fusion(f32[2,8,14,16,1000]{4,3,2,1,0:T(8,128)S(1)} %slice_add_fusion.3, f32[8,14,14]{2,1,0:T(8,128)S(1)} %broadcast_multiply_fusion, f32[14]{0:T(128)S(1)} %get-tuple-element.23, f32[14]{0:T(128)S(1)} %get-tuple-element.24), kind=kLoop, calls=%fused_computation.5 | loop fusion | flops 18816000 | bytes 50182384 | tf_op jit(solution)/shard_map/div | solution.py:82
  173.5 14.4 %div.64 = f32[3136,1000]{1,0:T(8,128)} reshape(f32[2,8,14,14,1000]{4,3,2,1,0:T(8,128)} %fusion.2) | data formatting | bytes 25088000 | tf_op jit(solution)/shard_map/div | solution.py:82
  187.8 13.3 %copy.22 = f32[3136,1000]{0,1:T(8,128)} copy(f32[3136,1000]{1,0:T(8,128)} %div.64) | data formatting | bytes 25088000 | tf_op jit(solution)/shard_map/div | solution.py:82
  201.2 5.3 %reduce_max.14 = f32[3136]{0:T(1024)S(1)} reduce(f32[3136,1000]{1,0:T(8,128)} %div.64, f32[]{:T(128)} %constant.26.clone.2), dimensions={1}, to_apply=%region_0.1.clone | reduce | flops 3132864 | bytes 12556548 | tf_op jit(solution)/shard_map/jit(log_softmax)/reduce_max | solution.py:82
  206.5 0.0 copy-start
  206.5 6.5 %exponential_reduce_fusion = f32[3136]{0:T(1024)S(1)} fusion(f32[3136,1000]{0,1:T(8,128)} %copy.22, f32[3136]{0:T(1024)S(1)} %reduce_max.14), kind=kLoop, calls=%fused_computation.10 | loop fusion | flops 6268864 | bytes 12569088 | tf_op jit(solution)/shard_map/jit(log_softmax)/reduce_sum | solution.py:82
  213.0 1.7 copy-done
  214.8 9.3 %multiply_reduce_fusion = (f32[]{:T(128)}, bf16[3136,1000]{0,1:T(8,128)(2,1)S(1)}) fusion(f32[3136,1000]{0,1:T(8,128)S(1)} %copy-done, f32[3136,1000]{0,1:T(8,128)} %copy-done.1, f32[3136]{0:T(1024)S(1)} %log.10, f32[3136]{0:T(1024)S(1)} %reduce_max.14, f32[3136]{0:T(1024)S(1)} %log.9, f32[3136]{0:T(1024)S(1)} %get-tuple-element.21), kind=kLoop, calls=%fused_computation.12 | loop fusion | flops 34496000 | bytes 31410180 | tf_op jit(solution)/shard_map/reduce_sum | solution.py:88
  224.0 0.0 copy-start.3
  224.0 2.7 copy-done.3
  226.7 10.7 %convolution_bitcast_fusion = f32[1024,1000]{0,1:T(8,128)} fusion(bf16[3136,1000]{0,1:T(8,128)(2,1)S(1)} %get-tuple-element.14, bf16[3136,1024]{1,0:T(8,128)(2,1)} %reshape.134), kind=kOutput, calls=%fused_computation.20 | convolution fusion | flops 6422528000 | bytes 16790528 | tf_op jit(solution)/shard_map/dot_general | solution.py:98
  237.5 0.0 all-reduce.2.cloned.1.call-update
  238.1 40.7 %psum.14 = f32[]{:T(128)} all-reduce(f32[]{:T(128)S(6)} %mul_shard_map.6), channel_id=1, replica_groups=mesh['ta'=2,'ha'=2,'wa'=8] {'ta','ha','wa'}, use_global_device_ids=true, to_apply=%region_3.5 | all-reduce | flops 1 | bytes 8 | tf_op jit(solution)/shard_map/psum | solution.py:101
  278.8 12.3 %convolution_convert_fusion = bf16[3136,1024]{1,0:T(8,128)(2,1)} fusion(bf16[3136,1000]{0,1:T(8,128)(2,1)} %copy-done.3, f32[1024,1000]{0,1:T(8,128)} %param.6), kind=kOutput, calls=%fused_computation.18 | convolution fusion | flops 6426763264 | bytes 16790528 | tf_op jit(solution)/shard_map/dot_general | solution.py:92
  291.1 10.0 %reshape.135 = bf16[2,8,14,14,1024]{4,3,2,1,0:T(8,128)(2,1)} reshape(bf16[3136,1024]{1,0:T(8,128)(2,1)} %convolution_convert_fusion) | data formatting | bytes 12845056 | tf_op jit(solution)/shard_map/reshape | solution.py:95
  301.1 10.7 %copy.23 = bf16[2,8,14,14,1024]{4,1,3,2,0:T(8,128)(2,1)} copy(bf16[2,8,14,14,1024]{4,3,2,1,0:T(8,128)(2,1)} %reshape.135) | data formatting | bytes 12845056
  311.8 68.5 %all-reduce.2.cloned.1.call-done = f32[1024,1000]{0,1:T(8,128)} async-done(((f32[1024,1000]{0,1:T(8,128)}), f32[1024,1000]{0,1:T(8,128)}) %all-reduce.2.cloned.1.call-update) | async-done | bytes 4096016 | tf_op jit(solution)/shard_map/psum | solution.py:101
  380.2 3.8 multiply_reduce_fusion.2
  384.8 1.5 multiply_subtract_fusion.1
  386.3 0.8 copy.24
  (7 shorter events, 0.1 us)
Async XLA Ops:
  7.2 373.1 %all-reduce.2.cloned.1.call-start = ((), (), s32[]{:S(2)}) async-start(), calls=%async_computation | async-start | bytes 8192000 | tf_op jit(solution)/shard_map/psum | solution.py:101
  7.2 14.5 %copy-start.2 = (bf16[2,8,14,14,1024]{4,1,3,2,0:T(8,128)(2,1)S(1)}, bf16[2,8,14,14,1024]{4,1,3,2,0:T(8,128)(2,1)}, u32[]{:S(2)}) copy-start(bf16[2,8,14,14,1024]{4,1,3,2,0:T(8,128)(2,1)} %param.4) | copy-start | bytes 19267588
  16.8 32.9 %collective-permute-start = (bf16[2,1,14,14,1000]{4,3,2,1,0:T(8,128)(2,1)}, bf16[2,1,14,14,1000]{4,3,2,1,0:T(8,128)(2,1)S(1)}, u32[]{:S(2)}, u32[]{:S(2)}) collective-permute-start(bf16[2,1,14,14,1000]{4,3,2,1,0:T(8,128)(2,1)} %copy.26), channel_id=1, source_target_pairs={{0,16},{1,17},{2,18},{3,19},{4,20},{5,21},{6,22},{7,23},{8,24},{9,... | collective-permute-start | bytes 2352008 | tf_op jit(solution)/shard_map/ppermute | solution.py:20
  20.4 43.5 %collective-permute-start.1 = (bf16[2,1,14,14,1000]{4,3,2,1,0:T(8,128)(2,1)}, bf16[2,1,14,14,1000]{4,3,2,1,0:T(8,128)(2,1)S(1)}, u32[]{:S(2)}, u32[]{:S(2)}) collective-permute-start(bf16[2,1,14,14,1000]{4,3,2,1,0:T(8,128)(2,1)} %copy.27), channel_id=1, source_target_pairs={{16,0},{17,1},{18,2},{19,3},{20,4},{21,5},{22,6},{23,7},{24,8},{25... | collective-permute-start | bytes 2352008 | tf_op jit(solution)/shard_map/ppermute | solution.py:23
  49.7 25.5 %copy-start.1 = (f32[3136,1000]{0,1:T(8,128)}, f32[3136,1000]{0,1:T(8,128)S(1)}, u32[]{:S(2)}) copy-start(f32[3136,1000]{0,1:T(8,128)S(1)} %get-tuple-element.22) | copy-start | bytes 37632004
  67.5 19.4 %collective-permute-start.2 = (bf16[2,10,1,14,1000]{4,3,2,1,0:T(8,128)(2,1)}, bf16[2,10,1,14,1000]{4,3,2,1,0:T(8,128)(2,1)S(1)}, u32[]{:S(2)}, u32[]{:S(2)}) collective-permute-start(bf16[2,10,1,14,1000]{4,3,2,1,0:T(8,128)(2,1)} %get-tuple-element.17), channel_id=1, source_target_pairs={{0,8},{1,9},{2,10},{3,11},{4,12},{5,13},{6,14},{7,15},{16,24},{17,... | collective-permute-start | bytes 1680008 | tf_op jit(solution)/shard_map/ppermute | solution.py:20
  71.7 19.6 %collective-permute-start.3 = (bf16[2,10,1,14,1000]{4,3,2,1,0:T(8,128)(2,1)}, bf16[2,10,1,14,1000]{4,3,2,1,0:T(8,128)(2,1)S(1)}, u32[]{:S(2)}, u32[]{:S(2)}) collective-permute-start(bf16[2,10,1,14,1000]{4,3,2,1,0:T(8,128)(2,1)} %get-tuple-element.18), channel_id=1, source_target_pairs={{8,0},{9,1},{10,2},{11,3},{12,4},{13,5},{14,6},{15,7},{24,16},{25,... | collective-permute-start | bytes 1680008 | tf_op jit(solution)/shard_map/ppermute | solution.py:23
  75.2 56.5 %slice-start = ((s8[9175040]{0:T(1024)(128)(4,1)}), s8[4194304]{0:T(1024)(128)(4,1)S(1)}, s32[]{:S(2)}) async-start(s8[9175040]{0:T(1024)(128)(4,1)} %bitcast.6), calls=%async_computation.1 | async-start | bytes 8388608
  75.2 56.5 %slice-start.1 = ((s8[9175040]{0:T(1024)(128)(4,1)}), s8[4194304]{0:T(1024)(128)(4,1)S(1)}, s32[]{:S(2)}) async-start(s8[9175040]{0:T(1024)(128)(4,1)} %bitcast.6), calls=%async_computation.2 | async-start | bytes 8388608
  97.4 34.3 %slice-start.2 = ((s8[9175040]{0:T(1024)(128)(4,1)}), s8[786432]{0:T(1024)(128)(4,1)S(1)}, s32[]{:S(2)}) async-start(s8[9175040]{0:T(1024)(128)(4,1)} %bitcast.6), calls=%async_computation.3 | async-start | bytes 1572864
  97.6 31.6 %collective-permute-start.4 = (bf16[2,10,16,1,1000]{4,2,3,1,0:T(8,128)(2,1)S(1)}, bf16[2,10,16,1,1000]{4,2,3,1,0:T(8,128)(2,1)S(1)}, u32[]{:S(2)}, u32[]{:S(2)}) collective-permute-start(bf16[2,10,16,1,1000]{4,2,3,1,0:T(8,128)(2,1)S(1)} %copy.18), channel_id=1, source_target_pairs={{0,1},{1,2},{2,3},{3,4},{4,5},{5,6},{6,7},{8,9},{9,10},{10,11},{11... | collective-permute-start | bytes 1920008 | tf_op jit(solution)/shard_map/ppermute | solution.py:20
  101.3 29.2 %collective-permute-start.5 = (bf16[2,10,16,1,1000]{4,2,3,1,0:T(8,128)(2,1)S(1)}, bf16[2,10,16,1,1000]{4,2,3,1,0:T(8,128)(2,1)S(1)}, u32[]{:S(2)}, u32[]{:S(2)}) collective-permute-start(bf16[2,10,16,1,1000]{4,2,3,1,0:T(8,128)(2,1)S(1)} %copy.19), channel_id=1, source_target_pairs={{1,0},{2,1},{3,2},{4,3},{5,4},{6,5},{7,6},{9,8},{10,9},{11,10},{12... | collective-permute-start | bytes 1920008 | tf_op jit(solution)/shard_map/ppermute | solution.py:23
  206.5 8.3 %copy-start = (f32[3136,1000]{0,1:T(8,128)S(1)}, f32[3136,1000]{0,1:T(8,128)}, u32[]{:S(2)}) copy-start(f32[3136,1000]{0,1:T(8,128)} %copy.22) | copy-start | bytes 37632004
  224.0 2.7 copy-start.3
Sparse Core Ops, SparseCore 0:
  237.6 142.5 all-reduce.1
where the time goes:
time: 402 us; the launch traced here: 394 us
  waiting for transfers between devices  111 us (28%)
  local copies, waits for them, and re-layouts  102 us (25%)
  other arithmetic  76.5 us (19%)
  blocking collectives  40.7 us (10%)
  matrix products  34.1 us (8%)
  between operations  15.9 us (4%)
  starting transfers between devices  14.1 us (4%)
    psum x1, waiting for transfers between devices, local(): lax.psum((local_grad, piece_objective), ('ta', 'ha', 'wa'))  68.5 us
    psum x1, blocking collectives, local(): lax.psum((local_grad, piece_objective), ('ta', 'ha', 'wa'))  40.7 us
    unnamed x21, local copies, waits for them, and re-layouts  39.4 us
    ppermute x3, waiting for transfers between devices, with_halo(): lax.ppermute(lax.slice_in_dim(block, block.shape[dim] - width, None, axis...  38.1 us
    div x2, local copies, waits for them, and re-layouts, local(): averaged_scores / sharpness_divisor  27.7 us
    add x2, other arithmetic, three_sum(): return first + middle + last  24.5 us
    dot_general x1, matrix products, local(): lax.dot_general(score_slope, head_bf, (((1,), (1,)), ((), ())), preferred...  12.3 us
    dot_general x1, matrix products, local(): jnp.dot(feat_rows, head_bf, preferred_element_type=jnp.float32)  11.1 us
  transfers between devices with their start and end apart: 7, of which 4 were waited for; matrix products, arithmetic and copies ran while one was open for 20% of the time, Pallas kernels for 0%

commit v1 on v0

v1 whole, which is shorter than its diff:
```python
import functools
import math

import jax
import jax.numpy as jnp
from jax import lax
from jax.experimental import pallas as pl
from jax.experimental.pallas import tpu as pltpu
from jax.sharding import PartitionSpec as P

WW = 14
WV = 28
AXES = ("ta", "ha", "wa")

sharpness_divisor = 2.0
learn_rate = 0.1
clip_norm = 1000.0
EXP2_SCALE = math.log2(math.e) / sharpness_divisor


def clip_of(columns):
    return (columns + WV - WW // 2) // WV


def round_up(value, multiple):
    return -(-value // multiple) * multiple


def exchange_halo(teacher):
    batch, frames, rows, columns, classes = teacher.shape
    ta, ha = lax.axis_index("ta"), lax.axis_index("ha")
    swap = [(0, 1), (1, 0)]
    count = lax.axis_size("wa")
    forward = [(i, i + 1) for i in range(count - 1)]
    backward = [(target, source) for source, target in forward]
    frame = jnp.where(ta == 0, teacher[:, -1], teacher[:, 0])
    frame = lax.ppermute(frame, "ta", swap)
    row = jnp.where(ha == 0, teacher[:, :, -1], teacher[:, :, 0])
    frame_row = jnp.where(ha == 0, frame[:, -1], frame[:, 0])
    row = lax.ppermute(jnp.concatenate([row, frame_row[:, None]], 1), "ha", swap)

    def column(at):
        own = jnp.concatenate([teacher[:, :, :, at], frame[:, None, :, at]], 1)
        return jnp.concatenate([own, row[:, :, at][:, :, None]], 2)

    left = lax.ppermute(column(columns - 1), "wa", forward)
    right = lax.ppermute(column(0), "wa", backward)
    return frame, row, left, right


def pool_weights(rows, columns, wide):
    ha, wa = lax.axis_index("ha"), lax.axis_index("wa")
    grid_wide = columns * lax.axis_size("wa")
    out = jnp.arange(rows * wide, dtype=jnp.int32)
    out_row, out_col = out // wide, out % wide
    halo_row = jnp.where(ha == 0, rows, -1)
    own_row = jnp.arange(rows * wide, dtype=jnp.int32) // wide
    own_col = jnp.arange(rows * wide, dtype=jnp.int32) % wide
    edge_rows = jnp.concatenate([jnp.arange(rows, dtype=jnp.int32), halo_row[None]])
    away = 1 << 20
    src_row = jnp.concatenate([own_row, jnp.full((columns,), 1, jnp.int32) * halo_row, edge_rows, edge_rows])
    src_col = jnp.concatenate(
        [
            jnp.where(own_col < columns, own_col, away),
            jnp.arange(columns, dtype=jnp.int32),
            jnp.full((rows + 1,), -1, jnp.int32),
            jnp.full((rows + 1,), columns, jnp.int32),
        ]
    )
    out_at, src_at = wa * columns + out_col, wa * columns + src_col
    near = (jnp.abs(out_row[:, None] - src_row[None]) <= 1) & (jnp.abs(out_col[:, None] - src_col[None]) <= 1)
    inside = (src_at >= 0) & (src_at < grid_wide)
    same = clip_of(out_at)[:, None] == clip_of(src_at)[None]
    weights = near & inside[None] & same & (out_col < columns)[:, None]
    return weights.astype(jnp.bfloat16)


def fused_kernel(
    frames, columns, flags, own, frame, halo, feats, pool, inverse, head, grad_out, head_grad, loss, sums, slopes, feat_keep
):
    batch_at, step = pl.program_id(0), pl.program_id(1)
    _, _, rows, wide, width = feats.shape
    tokens = rows * wide
    classes = head.shape[1]

    def planar(cells_ref_value, halo_value):
        keep = lax.broadcasted_iota(jnp.int32, cells_ref_value.shape, 1) < columns
        cells = jnp.where(keep, cells_ref_value, jnp.zeros_like(cells_ref_value)).reshape(tokens, classes)
        part = jnp.dot(pool[:, :tokens], cells, preferred_element_type=jnp.float32)
        return part + jnp.dot(pool[:, tokens:], halo_value, preferred_element_type=jnp.float32)

    @pl.when((step == 0) & (batch_at == 0))
    def _():
        loss[...] = jnp.zeros_like(loss)

    @pl.when(step == 0)
    def _():
        sums[2] = planar(frame[0], halo[0, frames]) * flags[0]

    @pl.when(step < frames)
    def _():
        sums[lax.rem(step, 3)] = planar(own[0, 0], halo[0, step])

    @pl.when(step == frames)
    def _():
        sums[frames % 3] = planar(frame[0], halo[0, frames]) * flags[1]

    @pl.when(step > 0)
    def _():
        at = step - 1
        keep = lax.broadcasted_iota(jnp.int32, (rows, wide, width), 1) < columns
        features = jnp.where(keep, feats[0, 0], jnp.zeros((rows, wide, width), feats.dtype)).reshape(tokens, width)
        student = jnp.dot(features, head[...], preferred_element_type=jnp.float32)
        pooled = (sums[0] + sums[1] + sums[2]) * inverse[0]
        teach = (pooled - jnp.max(pooled, -1, keepdims=True)) * EXP2_SCALE
        learn = (student - jnp.max(student, -1, keepdims=True)) * EXP2_SCALE
        teach_exp, learn_exp = jnp.exp2(teach), jnp.exp2(learn)
        teach_sum = jnp.sum(teach_exp, -1, keepdims=True)
        learn_sum = jnp.sum(learn_exp, -1, keepdims=True)
        cross = jnp.sum(teach_exp * (teach - learn), -1, keepdims=True)
        kl = math.log(2.0) * cross / teach_sum + jnp.log(learn_sum) - jnp.log(teach_sum)
        valid = lax.rem(lax.broadcasted_iota(jnp.int32, (tokens, 1), 0), wide) < columns
        kl = jnp.sum(jnp.where(valid, kl, 0.0), axis=0, keepdims=True)
        loss[...] += sharpness_divisor * sharpness_divisor * kl
        slope = learn_exp * (sharpness_divisor / learn_sum) - teach_exp * (sharpness_divisor / teach_sum)
        slope = slope.astype(jnp.bfloat16)
        grad = lax.dot_general(slope, head[...], (((1,), (1,)), ((), ())), preferred_element_type=jnp.float32)
        grad_out[0, 0] = grad.astype(grad_out.dtype).reshape(rows, wide, width)
        where = pl.ds(pl.multiple_of((batch_at * frames + at) * tokens, 16), tokens)
        slopes[where] = slope
        feat_keep[where] = features

    @pl.when((step == frames) & (batch_at == pl.num_programs(0) - 1))
    def _():
        chunk = 256

        @pl.loop(0, width // chunk)
        def _(i):
            part = pl.ds(pl.multiple_of(i * chunk, chunk), chunk)
            head_grad[part] = lax.dot_general(
                feat_keep[:, part], slopes[...], (((0,), (0,)), ((), ())), preferred_element_type=jnp.float32
            )


def local(features, teacher, head_weight):
    batch, frames, rows, columns, width = features.shape
    classes = teacher.shape[-1]
    wide = round_up(columns, 16)
    tokens = rows * wide
    ta, ha, wa = (lax.axis_index(axis) for axis in AXES)
    frame, row, left, right = exchange_halo(teacher)
    halo = jnp.concatenate([row, left, right], axis=2)
    pool = pool_weights(rows, columns, wide)
    frame_at = ta * frames + jnp.arange(frames, dtype=jnp.int32)
    row_at = ha * rows + jnp.arange(rows, dtype=jnp.int32)
    column_at = wa * columns + jnp.arange(wide, dtype=jnp.int32)

    def edge_count(position, length):
        return 3.0 - (position == 0).astype(jnp.float32) - (position == length - 1).astype(jnp.float32)

    own_clip = clip_of(column_at)
    left_ok = (column_at > 0) & (clip_of(column_at - 1) == own_clip)
    right_ok = (column_at < columns * lax.axis_size("wa") - 1) & (clip_of(column_at + 1) == own_clip)
    counts = (
        edge_count(frame_at, frames * lax.axis_size("ta"))[:, None, None]
        * edge_count(row_at, rows * lax.axis_size("ha"))[None, :, None]
        * (1.0 + left_ok.astype(jnp.float32) + right_ok.astype(jnp.float32))[None, None]
    )
    inverse = (1.0 / counts).reshape(frames, tokens, 1)
    flags = jnp.stack([(ta == 1), (ta == 0)]).astype(jnp.float32)
    head_bf = head_weight.astype(jnp.bfloat16)
    lag = lambda b, i: (b, jnp.maximum(i - 1, 0), 0, 0, 0)
    whole = lambda b, i: (0, 0)
    feature_grad, local_grad, loss = pl.pallas_call(
        functools.partial(fused_kernel, frames, columns),
        grid=(batch, frames + 1),
        in_specs=[
            pl.BlockSpec(memory_space=pltpu.SMEM),
            pl.BlockSpec((1, 1, rows, wide, classes), lambda b, i: (b, jnp.minimum(i, frames - 1), 0, 0, 0)),
            pl.BlockSpec((1, rows, wide, classes), lambda b, i: (b, 0, 0, 0)),
            pl.BlockSpec((1,) + halo.shape[1:], lambda b, i: (b, 0, 0, 0)),
            pl.BlockSpec((1, 1, rows, wide, width), lag),
            pl.BlockSpec(pool.shape, whole),
            pl.BlockSpec((1, tokens, 1), lambda b, i: (jnp.maximum(i - 1, 0), 0, 0)),
            pl.BlockSpec(head_bf.shape, whole),
        ],
        out_specs=[
            pl.BlockSpec((1, 1, rows, wide, width), lag),
            pl.BlockSpec((width, classes), whole),
            pl.BlockSpec((1, 1), whole),
        ],
        out_shape=[
            jax.ShapeDtypeStruct(features.shape, features.dtype),
            jax.ShapeDtypeStruct((width, classes), jnp.float32),
            jax.ShapeDtypeStruct((1, 1), jnp.float32),
        ],
        scratch_shapes=[
            pltpu.VMEM((3, tokens, classes), jnp.float32),
            pltpu.VMEM((batch * frames * tokens, classes), jnp.bfloat16),
            pltpu.VMEM((batch * frames * tokens, width), jnp.bfloat16),
        ],
        compiler_params=pltpu.CompilerParams(vmem_limit_bytes=60 * 1024 * 1024),
    )(flags, teacher, frame, halo, features, pool, inverse, head_bf)
    owned = width // lax.axis_size(AXES)
    mine = lax.psum_scatter(local_grad, AXES, scatter_dimension=0, tiled=True)
    squares, loss = lax.psum((jnp.sum(mine * mine), loss[0, 0]), AXES)
    clip = jnp.minimum(1.0, clip_norm / (jnp.sqrt(squares) + 1e-06))
    weight_rows = lax.dynamic_slice_in_dim(head_weight, lax.axis_index(AXES) * owned, owned, 0)
    return feature_grad, loss, weight_rows - learn_rate * clip * mine


def solution(mesh):
    assert mesh.shape["ta"] == 2 and mesh.shape["ha"] == 2
    placed = (P(None, "ta", "ha", "wa", None), P(None, "ta", "ha", "wa", None), P())
    return jax.shard_map(
        local,
        mesh=mesh,
        in_specs=placed,
        out_specs=(P(None, "ta", "ha", "wa", None), P(), P(AXES, None)),
        check_vma=False,
    )
```

time: 402 us -> 343 us (0.85); the launches traced: 394 us -> 341 us
  other arithmetic: 76.5 us -> 16.5 us
  Pallas kernels: 0 us -> 53.7 us
  local copies, waits for them, and re-layouts: 102 us -> 51.1 us
  waiting for transfers between devices: 111 us -> 153 us
  matrix products: 34.1 us -> 0 us
  starting transfers between devices: 14.1 us -> 9.02 us
    reduce_scatter x0 -> x1, waiting for transfers between devices: none -> 141 us  [local(): mine = lax.psum_scatter(local_grad, AXES, scatter_dimension=0, tiled=True)]
    psum x1 -> x0, waiting for transfers between devices: 68.5 us -> none  [local(): lax.psum((local_grad, piece_objective), ('ta', 'ha', 'wa'))]
    pallas_call x0 -> x1, Pallas kernels: none -> 53.7 us  [local(): pl.pallas_call(functools.partial(fused_kernel, frames, columns), grid=(ba...]
    dot_general x3 -> x0, matrix products: 34.1 us -> none  [the longest x1 12.3 us: local(): lax.dot_general(score_slope, head_bf, (((1,), (1,)), ((), ())), preferred...]
    ppermute x6 -> x4, waiting for transfers between devices: 42.6 us -> 11.3 us  [the longest x1 11.3 us: exchange_halo(): lax.ppermute(jnp.concatenate([row, frame_row[:, None]], 1), 'ha', swap)]
    div x2 -> x0, local copies, waits for them, and re-layouts: 27.7 us -> none  [local(): averaged_scores / sharpness_divisor]
    add x3 -> x1, other arithmetic: 24.5 us -> 0.02 us  [local(): 1.0 + left_ok.astype(jnp.float32) + right_ok.astype(jnp.float32)]
    reduce_sum x4 -> x1, other arithmetic: 21.7 us -> 1.54 us  [local(): squares, loss = lax.psum((jnp.sum(mine * mine), loss[0, 0]), AXES)]
  transfers between devices with their start and end apart: 7 -> 5, of which waited for: 4 -> 2; matrix products, arithmetic and copies ran while one was open for 20% -> 14% of each run, Pallas kernels for 0% -> 0%
where the time goes in v1:
time: 343 us; the launch traced here: 341 us
  waiting for transfers between devices  153 us (45%)
  Pallas kernels  53.7 us (16%)
  local copies, waits for them, and re-layouts  51.1 us (15%)
  blocking collectives  42.9 us (13%)
  other arithmetic  16.5 us (5%)
  between operations  15 us (4%)
  starting transfers between devices  9.02 us (3%)
    reduce_scatter x1, waiting for transfers between devices, local(): mine = lax.psum_scatter(local_grad, AXES, scatter_dimension=0, tiled=True)  141 us
    pallas_call x1, Pallas kernels, local(): pl.pallas_call(functools.partial(fused_kernel, frames, columns), grid=(ba...  53.7 us
    psum x1, blocking collectives, local(): squares, loss = lax.psum((jnp.sum(mine * mine), loss[0, 0]), AXES)  42.9 us
    unnamed x10, local copies, waits for them, and re-layouts  30.9 us
    ppermute x1, waiting for transfers between devices, exchange_halo(): lax.ppermute(jnp.concatenate([row, frame_row[:, None]], 1), 'ha', swap)  11.3 us
    slice x1, local copies, waits for them, and re-layouts, exchange_halo(): frame = jnp.where(ta == 0, teacher[:, -1], teacher[:, 0])  8.07 us
  transfers between devices with their start and end apart: 5, of which 2 were waited for; matrix products, arithmetic and copies ran while one was open for 14% of the time, Pallas kernels for 0%

profile of v1, /device:TPU:0, one launch (start us, length us, event | category | flops | bytes accessed | tf_op | source)
XLA Modules:
  0.0 340.8 jit_solution(7598176049425625310)
XLA Ops:
  7.2 0.0 reduce-scatter.2.cloned.1.call-start
  7.2 8.1 %fusion.17 = (bf16[2,1,14,14,1000]{4,1,3,2,0:T(2,128)(2,1)S(1)}, bf16[2,1,14,14,1000]{4,1,3,2,0:T(2,128)(2,1)S(1)}) fusion(bf16[2,8,14,14,1000]{4,1,3,2,0:T(8,128)(2,1)} %param.4), kind=kLoop, calls=%fused_computation.60 | loop fusion | bytes 3136000 | tf_op jit(solution)/shard_map/slice | solution.py:36
  15.3 3.0 fusion
  18.3 0.5 collective-permute-start
  18.8 0.1 pad_add_fusion
  18.9 0.1 compare_and_fusion
  19.0 1.2 fusion.16
  20.3 1.2 fusion.15
  21.5 1.2 fusion.1
  22.7 0.0 collective-permute-done
  22.7 0.0 copy-start.1
  22.7 0.1 broadcast_select_fusion.2
  22.8 0.7 pad_maximum_fusion.3
  23.5 2.6 collective-permute-start.1
  26.1 0.5 copy.85
  26.5 0.5 copy.84
  27.0 0.1 broadcast_multiply_fusion
  27.1 0.1 slice_bitcast_fusion.1
  27.2 11.3 %collective-permute-done.1 = bf16[2,9,14,1000]{3,0,2,1:T(2,128)(2,1)S(1)} collective-permute-done((bf16[2,9,14,1000]{3,0,2,1:T(2,128)(2,1)S(1)}, bf16[2,9,14,1000]{3,0,2,1:T(2,128)(2,1)S(1)}, u32[]{:S(2)}, u32[]{:S(2)}) %collective-permute-start.1) | collective-permute-done | bytes 504032 | tf_op jit(solution)/shard_map/ppermute | solution.py:40
  38.5 0.1 fusion.18
  38.5 1.6 pad_maximum_fusion.1
  40.2 4.5 %collective-permute-start.2 = (bf16[2,9,15,1000]{3,0,2,1:T(2,128)(2,1)}, bf16[2,9,15,1000]{3,0,2,1:T(2,128)(2,1)}, u32[]{:S(2)}, u32[]{:S(2)}) collective-permute-start(bf16[2,9,15,1000]{3,0,2,1:T(2,128)(2,1)} %pad_maximum_fusion.1), channel_id=1, source_target_pairs={{0,1},{1,2},{2,3},{3,4},{4,5},{5,6},{6,7},{8,9},{9,10},{10,11},{11... | collective-permute-start | bytes 1620008 | tf_op jit(solution)/shard_map/ppermute | solution.py:46
  44.6 1.6 pad_maximum_fusion.2
  46.3 1.5 collective-permute-start.3
  47.8 0.6 add_convert_fusion.flags
  48.4 9.4 %copy.63.own = bf16[2,8,14,14,1000]{4,3,2,1,0:T(8,128)(2,1)} copy(bf16[2,8,14,14,1000]{4,1,3,2,0:T(8,128)(2,1)} %param.4) | data formatting | bytes 12544000 | tf_op args[1]
  57.8 0.0 copy-done.1
  57.8 0.1 mul.83
  57.9 0.5 mul.95
  58.4 0.1 mul.86
  58.5 0.0 copy-start
  58.5 9.7 %copy.65.feats = bf16[2,8,14,14,1024]{4,3,2,1,0:T(8,128)(2,1)} copy(bf16[2,8,14,14,1024]{4,1,3,2,0:T(8,128)(2,1)} %param.3) | data formatting | bytes 12845056 | tf_op args[0]
  68.2 0.0 copy-done
  68.2 0.3 convert_element_type.59
  68.5 2.8 copy.66.head
  71.3 0.1 concatenate.39
  71.4 1.0 fusion.6.pool
  72.3 1.2 multiply_divide_fusion.inverse
  73.5 2.3 copy.64.frame
  75.8 0.1 copy.57
  75.9 0.0 collective-permute-done.2
  75.9 1.2 copy.58
  77.1 0.0 collective-permute-done.3
  77.1 1.2 copy.59
  78.3 1.8 pad_maximum_fusion.halo
  80.1 53.7 %shard_map.58 = (bf16[2,8,14,14,1024]{4,3,2,1,0:T(8,128)(2,1)}, f32[1024,1000]{1,0:T(8,128)}, f32[1,1]{1,0:T(1,128)}) custom-call(f32[2]{0:T(128)} %add_convert_fusion.flags, bf16[2,8,14,14,1000]{4,3,2,1,0:T(8,128)(2,1)} %copy.63.own, bf16[2,14,14,1000]{3,2,1,0:T(8,128)(2,1)} %copy.64.frame, bf16[2,9,44,1000]{3,2,1,0:T(8,128)(2,1)} %pad_maximum_fusion.halo, ...), custom_call_target="tpu_custom_call" | custom-call | tf_op jit(solution)/shard_map/pallas_call | solution.py:174
  133.9 0.0 reduce-scatter.2.cloned.1.call-update
  133.9 1.2 constant_dynamic-slice_fusion
  135.1 0.2 copy.75
  135.3 10.7 %copy.68 = bf16[2,8,14,14,1024]{4,1,3,2,0:T(8,128)(2,1)} copy(bf16[2,8,14,14,1024]{4,3,2,1,0:T(8,128)(2,1)} %get-tuple-element.18) | data formatting | bytes 12845056
  146.0 141.2 %reduce-scatter.2.cloned.1.call-done = f32[32,1000]{1,0:T(8,128)} async-done(((f32[1024,1000]{1,0:T(8,128)}), f32[32,1000]{1,0:T(8,128)}) %reduce-scatter.2.cloned.1.call-update) | async-done | bytes 128016 | tf_op jit(solution)/shard_map/reduce_scatter | solution.py:205
  287.2 1.5 multiply_reduce_fusion
  288.8 42.9 %all-reduce = (f32[]{:T(128)}, f32[]{:T(128)}) all-reduce(f32[]{:T(128)} %bitcast.9, f32[]{:T(128)} %multiply_reduce_fusion), channel_id=1, replica_groups=mesh['ta'=2,'ha'=2,'wa'=8] {'ta','ha','wa'}, use_global_device_ids=true, to_apply=%region_0.1 | all-reduce | flops 2 | bytes 16 | tf_op jit(solution)/shard_map/psum | solution.py:206
  332.4 1.6 multiply_subtract_fusion
  (13 shorter events, 0.1 us)
Async XLA Ops:
  7.2 280.1 %reduce-scatter.2.cloned.1.call-start = ((), (), s32[]{:S(2)}) async-start(), calls=%async_computation.1 | async-start | bytes 4325376 | tf_op jit(solution)/shard_map/reduce_scatter | solution.py:205
  18.3 4.4 %collective-permute-start = (bf16[2,14,14,1000]{3,0,2,1:T(2,128)(2,1)}, bf16[2,14,14,1000]{3,0,2,1:T(2,128)(2,1)S(1)}, u32[]{:S(2)}, u32[]{:S(2)}) collective-permute-start(bf16[2,14,14,1000]{3,0,2,1:T(2,128)(2,1)} %fusion), channel_id=1, source_target_pairs={{0,16},{16,0},{1,17},{17,1},{2,18},{18,2},{3,19},{19,3},{4,20},{20... | collective-permute-start | bytes 2352008 | tf_op jit(solution)/shard_map/ppermute | solution.py:37
  22.7 35.1 %copy-start.1 = (bf16[2,14,14,1000]{3,0,2,1:T(2,128)(2,1)}, bf16[2,14,14,1000]{3,0,2,1:T(2,128)(2,1)S(1)}, u32[]{:S(2)}) copy-start(bf16[2,14,14,1000]{3,0,2,1:T(2,128)(2,1)S(1)} %collective-permute-done) | copy-start | bytes 2352004
  23.5 15.0 %collective-permute-start.1 = (bf16[2,9,14,1000]{3,0,2,1:T(2,128)(2,1)S(1)}, bf16[2,9,14,1000]{3,0,2,1:T(2,128)(2,1)S(1)}, u32[]{:S(2)}, u32[]{:S(2)}) collective-permute-start(bf16[2,9,14,1000]{3,0,2,1:T(2,128)(2,1)S(1)} %pad_maximum_fusion.3), channel_id=1, source_target_pairs={{0,8},{8,0},{1,9},{9,1},{2,10},{10,2},{3,11},{11,3},{4,12},{12,4},... | collective-permute-start | bytes 1512008 | tf_op jit(solution)/shard_map/ppermute | solution.py:40
  40.2 35.8 %collective-permute-start.2 = (bf16[2,9,15,1000]{3,0,2,1:T(2,128)(2,1)}, bf16[2,9,15,1000]{3,0,2,1:T(2,128)(2,1)}, u32[]{:S(2)}, u32[]{:S(2)}) collective-permute-start(bf16[2,9,15,1000]{3,0,2,1:T(2,128)(2,1)} %pad_maximum_fusion.1), channel_id=1, source_target_pairs={{0,1},{1,2},{2,3},{3,4},{4,5},{5,6},{6,7},{8,9},{9,10},{10,11},{11... | collective-permute-start | bytes 1620008 | tf_op jit(solution)/shard_map/ppermute | solution.py:46
  46.3 30.9 %collective-permute-start.3 = (bf16[2,9,15,1000]{3,0,2,1:T(2,128)(2,1)}, bf16[2,9,15,1000]{3,0,2,1:T(2,128)(2,1)}, u32[]{:S(2)}, u32[]{:S(2)}) collective-permute-start(bf16[2,9,15,1000]{3,0,2,1:T(2,128)(2,1)} %pad_maximum_fusion.2), channel_id=1, source_target_pairs={{1,0},{2,1},{3,2},{4,3},{5,4},{6,5},{7,6},{9,8},{10,9},{11,10},{12... | collective-permute-start | bytes 1620008 | tf_op jit(solution)/shard_map/ppermute | solution.py:47
  58.5 9.7 %copy-start = (f32[1024,1000]{0,1:T(8,128)S(1)}, f32[1024,1000]{0,1:T(8,128)}, u32[]{:S(2)}) copy-start(f32[1024,1000]{0,1:T(8,128)} %param.5) | copy-start | bytes 12288004
Sparse Core Ops, SparseCore 0:
  134.0 153.1 reduce-scatter.1

commit v2 on v1

--- a/solution.py
+++ b/solution.py
@@ -139,7 +139,124 @@
             part = pl.ds(pl.multiple_of(i * chunk, chunk), chunk)
             head_grad[part] = lax.dot_general(
                 feat_keep[:, part], slopes[...], (((0,), (0,)), ((), ())), preferred_element_type=jnp.float32
-            )
+            ).astype(head_grad.dtype)
+
+
+def reduce_kernel(peers, partial, local_loss, weight, new_weight, loss, landed, summed, arrived, stats, stat_in, stat_out, gathered,
+                  core_send, core_recv, peer_send, peer_recv, stat_send, stat_recv, pair_sem):
+    ta, ha, wa = (lax.axis_index(axis) for axis in AXES)
+    per_row = lax.axis_size("wa")
+    me = ha * per_row + wa
+    other = {"ta": 1 - ta}
+
+    def peer(k):
+        return lax.rem(me + k, peers)
+
+    def place(at):
+        return {"ha": at // per_row, "wa": lax.rem(at, per_row)}
+
+    barrier = pltpu.get_barrier_semaphore()
+    pl.semaphore_signal(barrier, inc=1, device_id=other, device_id_type=pl.DeviceIdType.MESH)
+
+    @pl.loop(1, peers)
+    def _(k):
+        pl.semaphore_signal(barrier, inc=1, device_id=place(peer(k)), device_id_type=pl.DeviceIdType.MESH)
+
+    pl.semaphore_wait(barrier, peers)
+
+    def to_core(k):
+        at = peer(k)
+        return pltpu.make_async_remote_copy(
+            src_ref=partial.at[1 - ta, at], dst_ref=landed.at[at], send_sem=core_send.at[lax.rem(k, peers)],
+            recv_sem=core_recv.at[lax.rem(k, peers)], device_id=other, device_id_type=pl.DeviceIdType.MESH)
+
+    def to_peer(k):
+        at = peer(k)
+        return pltpu.make_async_remote_copy(
+            src_ref=summed.at[at], dst_ref=arrived.at[k], send_sem=peer_send.at[k],
+            recv_sem=peer_recv.at[k], device_id=place(at), device_id_type=pl.DeviceIdType.MESH)
+
+    def stat_to(k):
+        return pltpu.make_async_remote_copy(
+            src_ref=stats, dst_ref=gathered.at[me], send_sem=stat_send.at[k],
+            recv_sem=stat_recv.at[k], device_id=place(peer(k)), device_id_type=pl.DeviceIdType.MESH)
+
+    @pl.loop(1, peers + 1)
+    def _(k):
+        to_core(k).start()
+
+    @pl.loop(1, peers)
+    def _(k):
+        at = peer(k)
+        to_core(k).wait_recv()
+        summed[at] = (partial[ta, at].astype(jnp.float32) + landed[at].astype(jnp.float32)).astype(summed.dtype)
+        to_peer(k).start()
+
+    to_core(peers).wait_recv()
+    new_weight[...] = partial[ta, me].astype(jnp.float32) + landed[me].astype(jnp.float32)
+
+    @pl.loop(1, peers)
+    def _(k):
+        to_peer(k).wait_recv()
+        new_weight[...] += arrived[k].astype(jnp.float32)
+
+    total = new_weight[...]
+    squares = jnp.sum(jnp.sum(total * total, axis=1, keepdims=True), axis=0, keepdims=True)
+    lane = lax.broadcasted_iota(jnp.int32, stat_out.shape, 1)
+    stat_out[...] = jnp.where(lane == 0, squares, local_loss[...])
+    pair = pltpu.make_async_remote_copy(
+        src_ref=stat_out, dst_ref=stat_in, send_sem=pair_sem.at[0], recv_sem=pair_sem.at[1],
+        device_id=other, device_id_type=pl.DeviceIdType.MESH)
+    pair.start()
+    pair.wait()
+    stats[...] = stat_out[...] + stat_in[...]
+    gathered[me] = stats[...]
+
+    @pl.loop(1, peers)
+    def _(k):
+        stat_to(k).start()
+
+    @pl.loop(1, peers)
+    def _(k):
+        stat_to(k).wait_recv()
+
+    both = jnp.sum(gathered[...], axis=0)
+    norm = jnp.sqrt(both[0:1, 0:1])
+    loss[...] = both[0:1, 1:2]
+    clip = jnp.minimum(1.0, clip_norm / (norm + 1e-06))
+    new_weight[...] = weight[...] - learn_rate * clip * new_weight[...]
+
+    @pl.loop(1, peers)
+    def _(k):
+        to_core(k).wait_send()
+        to_peer(k).wait_send()
+        stat_to(k).wait_send()
+
+    to_core(peers).wait_send()
+
+
+def reduce_and_update(local_grad, local_loss, weight_rows):
+    owned, classes = weight_rows.shape
+    peers = lax.axis_size(("ha", "wa"))
+    partial = local_grad.reshape(2, peers, owned, classes)
+    vmem = pl.BlockSpec(memory_space=pltpu.VMEM)
+    dma = pltpu.SemaphoreType.DMA
+    slots = pltpu.VMEM((peers, owned, classes), local_grad.dtype)
+    return pl.pallas_call(
+        functools.partial(reduce_kernel, peers),
+        in_specs=[vmem] * 3,
+        out_specs=[vmem] * 2,
+        out_shape=[
+            jax.ShapeDtypeStruct((owned, classes), jnp.float32),
+            jax.ShapeDtypeStruct((1, 1), jnp.float32),
+        ],
+        scratch_shapes=[slots, slots, slots]
+        + [pltpu.VMEM((8, 128), jnp.float32)] * 3
+        + [pltpu.VMEM((peers, 8, 128), jnp.float32)]
+        + [dma((peers,))] * 6
+        + [dma((2,))],
+        compiler_params=pltpu.CompilerParams(collective_id=0, has_side_effects=True),
+    )(partial, local_loss, weight_rows)
 
 
 def local(features, teacher, head_weight):
@@ -191,7 +308,7 @@
         ],
         out_shape=[
             jax.ShapeDtypeStruct(features.shape, features.dtype),
-            jax.ShapeDtypeStruct((width, classes), jnp.float32),
+            jax.ShapeDtypeStruct((width, classes), jnp.bfloat16),
             jax.ShapeDtypeStruct((1, 1), jnp.float32),
         ],
         scratch_shapes=[
@@ -202,11 +319,9 @@
         compiler_params=pltpu.CompilerParams(vmem_limit_bytes=60 * 1024 * 1024),
     )(flags, teacher, frame, halo, features, pool, inverse, head_bf)
     owned = width // lax.axis_size(AXES)
-    mine = lax.psum_scatter(local_grad, AXES, scatter_dimension=0, tiled=True)
-    squares, loss = lax.psum((jnp.sum(mine * mine), loss[0, 0]), AXES)
-    clip = jnp.minimum(1.0, clip_norm / (jnp.sqrt(squares) + 1e-06))
     weight_rows = lax.dynamic_slice_in_dim(head_weight, lax.axis_index(AXES) * owned, owned, 0)
-    return feature_grad, loss, weight_rows - learn_rate * clip * mine
+    new_weight, loss = reduce_and_update(local_grad, loss, weight_rows)
+    return feature_grad, loss[0, 0], new_weight
 
 
 def solution(mesh):

time: 343 us -> 188 us (0.55)
  waiting for transfers between devices: 153 us -> 11.3 us
  blocking collectives: 42.9 us -> 0 us
  Pallas kernels: 53.7 us -> 95.4 us
  between operations: 15 us -> 2.6 us
    reduce_scatter x1 -> x0, waiting for transfers between devices: 141 us -> none  [local(): mine = lax.psum_scatter(local_grad, AXES, scatter_dimension=0, tiled=True)]
    psum x1 -> x0, blocking collectives: 42.9 us -> none  [local(): squares, loss = lax.psum((jnp.sum(mine * mine), loss[0, 0]), AXES)]
    pallas_call x0 -> x1, Pallas kernels: none -> 42.3 us  [reduce_and_update(): pl.pallas_call(functools.partial(reduce_kernel, peers), in_specs=[vmem] *...]
    unnamed x10 -> x27, local copies, waits for them, and re-layouts: 30.9 us -> 32.3 us
  transfers between devices with their start and end apart: 5 -> 4, of which waited for: 2 -> 1; matrix products, arithmetic and copies ran while one was open for 14% -> 22% of each run, Pallas kernels for 0% -> 0%
where the time goes in v2:
time: 188 us
  Pallas kernels  95.4 us (51%)
  local copies, waits for them, and re-layouts  53.1 us (28%)
  other arithmetic  16.2 us (9%)
  waiting for transfers between devices  11.3 us (6%)
  starting transfers between devices  8.97 us (5%)
  between operations  2.6 us (1%)
    pallas_call x1, Pallas kernels, local(): pl.pallas_call(functools.partial(fused_kernel, frames, columns), grid=(ba...  53.1 us
    pallas_call x1, Pallas kernels, reduce_and_update(): pl.pallas_call(functools.partial(reduce_kernel, peers), in_specs=[vmem] *...  42.3 us
    unnamed x27, local copies, waits for them, and re-layouts  32.3 us
    ppermute x1, waiting for transfers between devices, exchange_halo(): lax.ppermute(jnp.concatenate([row, frame_row[:, None]], 1), 'ha', swap)  11.3 us
    slice x1, local copies, waits for them, and re-layouts, exchange_halo(): frame = jnp.where(ta == 0, teacher[:, -1], teacher[:, 0])  8.07 us
    ppermute x1, starting transfers between devices, exchange_halo(): left = lax.ppermute(column(columns - 1), 'wa', forward)  4.48 us
  transfers between devices with their start and end apart: 4, of which 1 were waited for; matrix products, arithmetic and copies ran while one was open for 22% of the time, Pallas kernels for 0%

profile of v2, /device:TPU:0, one launch (start us, length us, event | category | flops | bytes accessed | tf_op | source)
XLA Modules:
  0.0 187.7 jit_solution(7270708923842527733)
XLA Ops:
  0.6 8.1 %fusion.17 = (bf16[2,1,14,14,1000]{4,1,3,2,0:T(2,128)(2,1)S(1)}, bf16[2,1,14,14,1000]{4,1,3,2,0:T(2,128)(2,1)S(1)}) fusion(bf16[2,8,14,14,1000]{4,1,3,2,0:T(8,128)(2,1)} %param.4), kind=kLoop, calls=%fused_computation.58 | loop fusion | bytes 3136000 | tf_op jit(solution)/shard_map/slice | solution.py:36
  8.7 3.0 %fusion = bf16[2,14,14,1000]{3,0,2,1:T(2,128)(2,1)} fusion(pred[]{:T(512)} %eq.71, bf16[2,1,14,14,1000]{4,1,3,2,0:T(2,128)(2,1)S(1)} %get-tuple-element.30, bf16[2,1,14,14,1000]{4,1,3,2,0:T(2,128)(2,1)S(1)} %get-tuple-element.29), kind=kLoop, calls=%fused_computation.4 | loop fusion | flops 392000 | bytes 2352001 | tf_op jit(solution)/shard_map/jit(_where)/select_n | solution.py:36
  11.7 0.5 collective-permute-start
  12.2 0.6 and_select_fusion.5
  12.8 0.1 pad_add_fusion
  12.9 0.7 compare_and_fusion
  13.5 0.6 and_select_fusion.3
  14.1 0.5 broadcast_compare_fusion
  14.6 0.6 fusion.14
  15.2 1.2 constant_dynamic-slice_fusion
  16.5 1.2 fusion.16
  17.7 1.2 fusion.15
  18.9 1.2 fusion.1
  20.1 0.0 collective-permute-done
  20.1 0.0 copy-start.1
  20.1 0.1 broadcast_select_fusion.2
  20.2 0.7 pad_maximum_fusion.3
  20.9 2.5 %collective-permute-start.1 = (bf16[2,9,14,1000]{3,0,2,1:T(2,128)(2,1)S(1)}, bf16[2,9,14,1000]{3,0,2,1:T(2,128)(2,1)S(1)}, u32[]{:S(2)}, u32[]{:S(2)}) collective-permute-start(bf16[2,9,14,1000]{3,0,2,1:T(2,128)(2,1)S(1)} %pad_maximum_fusion.3), channel_id=1, source_target_pairs={{0,8},{8,0},{1,9},{9,1},{2,10},{10,2},{3,11},{11,3},{4,12},{12,4},... | collective-permute-start | bytes 1512008 | tf_op jit(solution)/shard_map/ppermute | solution.py:40
  23.5 0.5 copy.84
  23.9 0.5 copy.83
  24.4 0.1 broadcast_multiply_fusion
  24.5 0.1 slice_bitcast_fusion.1
  24.6 11.3 %collective-permute-done.1 = bf16[2,9,14,1000]{3,0,2,1:T(2,128)(2,1)S(1)} collective-permute-done((bf16[2,9,14,1000]{3,0,2,1:T(2,128)(2,1)S(1)}, bf16[2,9,14,1000]{3,0,2,1:T(2,128)(2,1)S(1)}, u32[]{:S(2)}, u32[]{:S(2)}) %collective-permute-start.1) | collective-permute-done | bytes 504032 | tf_op jit(solution)/shard_map/ppermute | solution.py:40
  35.9 0.1 fusion.18
  35.9 1.7 pad_maximum_fusion.1
  37.6 4.5 %collective-permute-start.2 = (bf16[2,9,15,1000]{3,0,2,1:T(2,128)(2,1)}, bf16[2,9,15,1000]{3,0,2,1:T(2,128)(2,1)}, u32[]{:S(2)}, u32[]{:S(2)}) collective-permute-start(bf16[2,9,15,1000]{3,0,2,1:T(2,128)(2,1)} %pad_maximum_fusion.1), channel_id=1, source_target_pairs={{0,1},{1,2},{2,3},{3,4},{4,5},{5,6},{6,7},{8,9},{9,10},{10,11},{11... | collective-permute-start | bytes 1620008 | tf_op jit(solution)/shard_map/ppermute | solution.py:46
  42.1 1.7 pad_maximum_fusion.2
  43.7 1.5 collective-permute-start.3
  45.2 0.6 add_convert_fusion.flags
  45.8 0.0 copy-done.1
  45.8 0.0 copy-done.2
  45.8 9.6 %copy.63.own = bf16[2,8,14,14,1000]{4,3,2,1,0:T(8,128)(2,1)} copy(bf16[2,8,14,14,1000]{4,1,3,2,0:T(8,128)(2,1)} %param.4) | data formatting | bytes 12544000 | tf_op args[1]
  55.4 0.0 copy-done
  55.4 0.3 convert_element_type.59
  55.7 0.1 mul.74
  55.8 0.5 mul.83
  56.3 0.7 mul.76
  57.0 0.1 mul.77
  57.1 9.5 %copy.65.feats = bf16[2,8,14,14,1024]{4,3,2,1,0:T(8,128)(2,1)} copy(bf16[2,8,14,14,1024]{4,1,3,2,0:T(8,128)(2,1)} %param.3) | data formatting | bytes 12845056 | tf_op args[0]
  66.6 0.0 copy-start.9
  66.6 2.8 %copy.66.head = bf16[1024,1000]{1,0:T(8,128)(2,1)} copy(bf16[1024,1000]{0,1:T(8,128)(2,1)S(1)} %convert_element_type.59) | data formatting | bytes 4096000 | tf_op jit(solution)/shard_map/convert_element_type | solution.py:288
  69.4 0.8 copy.75.weight
  70.2 0.0 copy-done.7
  70.2 0.1 concatenate.39
  70.3 0.0 copy-done.5
  70.3 0.0 copy-done.6
  70.3 0.0 copy-done.8
  70.3 0.0 copy-done.9
  70.3 0.9 fusion.6.pool
  71.3 1.1 multiply_divide_fusion.inverse
  72.4 2.3 %copy.64.frame = bf16[2,14,14,1000]{3,2,1,0:T(8,128)(2,1)} copy(bf16[2,14,14,1000]{3,0,2,1:T(2,128)(2,1)} %copy-done.1) | data formatting | bytes 1568000 | tf_op jit(solution)/shard_map/ppermute | solution.py:37
  74.7 0.0 copy-done.3
  74.7 0.1 copy.57
  74.8 0.0 collective-permute-done.2
  74.8 1.2 copy.58
  76.0 0.0 collective-permute-done.3
  76.0 1.2 copy.59
  77.2 1.9 pad_maximum_fusion.halo
  79.1 53.1 %shard_map.58 = (bf16[2,8,14,14,1024]{4,3,2,1,0:T(8,128)(2,1)}, bf16[1024,1000]{1,0:T(8,128)(2,1)}, f32[1,1]{1,0:T(1,128)}) custom-call(f32[2]{0:T(128)} %add_convert_fusion.flags, bf16[2,8,14,14,1000]{4,3,2,1,0:T(8,128)(2,1)} %copy.63.own, bf16[2,14,14,1000]{3,2,1,0:T(8,128)(2,1)} %copy.64.frame, bf16[2,9,44,1000]{3,2,1,0:T(8,128)(2,1)} %pad_maximum_fusion.halo, ...), custom_call_target="tpu_custom_call" | custom-call | tf_op jit(solution)/shard_map/pallas_call | solution.py:291
  132.2 42.3 %shard_map.59 = (f32[32,1000]{1,0:T(8,128)}, f32[1,1]{1,0:T(1,128)}) custom-call(bf16[2,16,32,1000]{3,2,1,0:T(8,128)(2,1)} %bitcast.19, f32[1,1]{1,0:T(1,128)} %get-tuple-element.10.local_loss, f32[32,1000]{1,0:T(8,128)} %copy.75.weight), custom_call_target="tpu_custom_call" | custom-call | tf_op jit(solution)/shard_map/pallas_call | solution.py:245
  174.5 0.0 copy-start.4
  174.5 10.7 %copy.68 = bf16[2,8,14,14,1024]{4,1,3,2,0:T(8,128)(2,1)} copy(bf16[2,8,14,14,1024]{4,3,2,1,0:T(8,128)(2,1)} %get-tuple-element.22) | data formatting | bytes 12845056
  185.9 0.0 copy-done.4
  185.9 0.7 copy.88
  (15 shorter events, 0.0 us)
Async XLA Ops:
  11.7 8.4 %collective-permute-start = (bf16[2,14,14,1000]{3,0,2,1:T(2,128)(2,1)}, bf16[2,14,14,1000]{3,0,2,1:T(2,128)(2,1)S(1)}, u32[]{:S(2)}, u32[]{:S(2)}) collective-permute-start(bf16[2,14,14,1000]{3,0,2,1:T(2,128)(2,1)} %fusion), channel_id=1, source_target_pairs={{0,16},{16,0},{1,17},{17,1},{2,18},{18,2},{3,19},{19,3},{4,20},{20... | collective-permute-start | bytes 2352008 | tf_op jit(solution)/shard_map/ppermute | solution.py:37
  20.1 25.7 %copy-start.1 = (bf16[2,14,14,1000]{3,0,2,1:T(2,128)(2,1)}, bf16[2,14,14,1000]{3,0,2,1:T(2,128)(2,1)S(1)}, u32[]{:S(2)}) copy-start(bf16[2,14,14,1000]{3,0,2,1:T(2,128)(2,1)S(1)} %collective-permute-done) | copy-start | bytes 2352004
  20.9 15.0 %collective-permute-start.1 = (bf16[2,9,14,1000]{3,0,2,1:T(2,128)(2,1)S(1)}, bf16[2,9,14,1000]{3,0,2,1:T(2,128)(2,1)S(1)}, u32[]{:S(2)}, u32[]{:S(2)}) collective-permute-start(bf16[2,9,14,1000]{3,0,2,1:T(2,128)(2,1)S(1)} %pad_maximum_fusion.3), channel_id=1, source_target_pairs={{0,8},{8,0},{1,9},{9,1},{2,10},{10,2},{3,11},{11,3},{4,12},{12,4},... | collective-permute-start | bytes 1512008 | tf_op jit(solution)/shard_map/ppermute | solution.py:40
  35.9 9.9 %copy-start.2 = (bf16[2,9,14,1000]{3,0,2,1:T(2,128)(2,1)}, bf16[2,9,14,1000]{3,0,2,1:T(2,128)(2,1)S(1)}, u32[]{:S(2)}) copy-start(bf16[2,9,14,1000]{3,0,2,1:T(2,128)(2,1)S(1)} %collective-permute-done.1) | copy-start | bytes 1512004
  37.6 37.2 %collective-permute-start.2 = (bf16[2,9,15,1000]{3,0,2,1:T(2,128)(2,1)}, bf16[2,9,15,1000]{3,0,2,1:T(2,128)(2,1)}, u32[]{:S(2)}, u32[]{:S(2)}) collective-permute-start(bf16[2,9,15,1000]{3,0,2,1:T(2,128)(2,1)} %pad_maximum_fusion.1), channel_id=1, source_target_pairs={{0,1},{1,2},{2,3},{3,4},{4,5},{5,6},{6,7},{8,9},{9,10},{10,11},{11... | collective-permute-start | bytes 1620008 | tf_op jit(solution)/shard_map/ppermute | solution.py:46
  43.7 32.3 %collective-permute-start.3 = (bf16[2,9,15,1000]{3,0,2,1:T(2,128)(2,1)}, bf16[2,9,15,1000]{3,0,2,1:T(2,128)(2,1)}, u32[]{:S(2)}, u32[]{:S(2)}) collective-permute-start(bf16[2,9,15,1000]{3,0,2,1:T(2,128)(2,1)} %pad_maximum_fusion.2), channel_id=1, source_target_pairs={{1,0},{2,1},{3,2},{4,3},{5,4},{6,5},{7,6},{9,8},{10,9},{11,10},{12... | collective-permute-start | bytes 1620008 | tf_op jit(solution)/shard_map/ppermute | solution.py:47
  45.8 9.6 %copy-start = (f32[1024,1000]{0,1:T(8,128)S(1)}, f32[1024,1000]{0,1:T(8,128)}, u32[]{:S(2)}) copy-start(f32[1024,1000]{0,1:T(8,128)} %param.5) | copy-start | bytes 12288004
  66.6 3.6 %copy-start.7 = (s32[224]{0:T(256)S(1)}, s32[224]{0:T(256)}, u32[]{:S(2)}) copy-start(s32[224]{0:T(256)} %and_select_fusion.5) | copy-start | bytes 2692
  66.6 3.7 %copy-start.5 = (s32[224]{0:T(256)S(1)}, s32[224]{0:T(256)}, u32[]{:S(2)}) copy-start(s32[224]{0:T(256)} %get-tuple-element.37) | copy-start | bytes 2692
  66.6 3.7 %copy-start.6 = (s32[224]{0:T(256)S(1)}, s32[224]{0:T(256)}, u32[]{:S(2)}) copy-start(s32[224]{0:T(256)} %get-tuple-element.38) | copy-start | bytes 2692
  66.6 3.7 %copy-start.8 = (pred[268]{0:T(512)(128)(4,1)S(1)}, pred[268]{0:T(512)(128)(4,1)}, u32[]{:S(2)}) copy-start(pred[268]{0:T(512)(128)(4,1)} %compare_and_fusion) | copy-start | bytes 808
  66.6 3.7 %copy-start.9 = (pred[224]{0:T(512)(128)(4,1)S(1)}, pred[224]{0:T(512)(128)(4,1)}, u32[]{:S(2)}) copy-start(pred[224]{0:T(512)(128)(4,1)} %broadcast_compare_fusion) | copy-start | bytes 676
  69.4 5.3 %copy-start.3 = (bf16[2,9,14,1000]{3,0,2,1:T(2,128)(2,1)S(1)}, bf16[2,9,14,1000]{3,0,2,1:T(2,128)(2,1)}, u32[]{:S(2)}) copy-start(bf16[2,9,14,1000]{3,0,2,1:T(2,128)(2,1)} %copy-done.2) | copy-start | bytes 1512004
  174.5 11.3 %copy-start.4 = (f32[32,1000]{1,0:T(8,128)S(1)}, f32[32,1000]{1,0:T(8,128)}, u32[]{:S(2)}) copy-start(f32[32,1000]{1,0:T(8,128)} %get-tuple-element.44) | copy-start | bytes 384004

commit v3 on v2

--- a/solution.py
+++ b/solution.py
@@ -22,94 +22,78 @@
     return (columns + WV - WW // 2) // WV
 
 
-def round_up(value, multiple):
-    return -(-value // multiple) * multiple
-
-
 def exchange_halo(teacher):
-    batch, frames, rows, columns, classes = teacher.shape
+    batch, rows, columns, frames, classes = teacher.shape
     ta, ha = lax.axis_index("ta"), lax.axis_index("ha")
     swap = [(0, 1), (1, 0)]
     count = lax.axis_size("wa")
     forward = [(i, i + 1) for i in range(count - 1)]
     backward = [(target, source) for source, target in forward]
-    frame = jnp.where(ta == 0, teacher[:, -1], teacher[:, 0])
-    frame = lax.ppermute(frame, "ta", swap)
-    row = jnp.where(ha == 0, teacher[:, :, -1], teacher[:, :, 0])
-    frame_row = jnp.where(ha == 0, frame[:, -1], frame[:, 0])
-    row = lax.ppermute(jnp.concatenate([row, frame_row[:, None]], 1), "ha", swap)
-
-    def column(at):
-        own = jnp.concatenate([teacher[:, :, :, at], frame[:, None, :, at]], 1)
-        return jnp.concatenate([own, row[:, :, at][:, :, None]], 2)
-
-    left = lax.ppermute(column(columns - 1), "wa", forward)
-    right = lax.ppermute(column(0), "wa", backward)
-    return frame, row, left, right
-
-
-def pool_weights(rows, columns, wide):
-    ha, wa = lax.axis_index("ha"), lax.axis_index("wa")
+
+    def facing_frame(cells):
+        facing = lax.broadcasted_iota(jnp.int32, cells.shape, cells.ndim - 2) == jnp.where(ta == 0, frames - 1, 0)
+        return jnp.sum(jnp.where(facing, cells, jnp.zeros_like(cells)), axis=-2)
+
+    row = lax.dynamic_slice_in_dim(teacher, jnp.where(ha == 0, rows - 1, 0), 1, 1)
+    row = lax.ppermute(row, "ha", swap)
+    frame = lax.ppermute(facing_frame(teacher), "ta", swap)
+    left = lax.ppermute(jnp.concatenate([teacher[:, :, -1], row[:, :, -1]], 1), "wa", forward)
+    right = lax.ppermute(jnp.concatenate([teacher[:, :, 0], row[:, :, 0]], 1), "wa", backward)
+    edges = jnp.concatenate([facing_frame(row[:, 0]), facing_frame(left), facing_frame(right)], 1)
+    edges = lax.ppermute(edges, "ta", swap)
+    frame = jnp.concatenate([frame, edges[:, None, :columns]], 1)
+    frame_left = edges[:, columns : columns + rows + 1, None]
+    frame_right = edges[:, columns + rows + 1 :, None]
+    return row, jnp.concatenate([left, right, frame, frame_left, frame_right], 2)
+
+
+def pool_weights(columns, frames):
+    ta, wa = lax.axis_index("ta"), lax.axis_index("wa")
     grid_wide = columns * lax.axis_size("wa")
-    out = jnp.arange(rows * wide, dtype=jnp.int32)
-    out_row, out_col = out // wide, out % wide
-    halo_row = jnp.where(ha == 0, rows, -1)
-    own_row = jnp.arange(rows * wide, dtype=jnp.int32) // wide
-    own_col = jnp.arange(rows * wide, dtype=jnp.int32) % wide
-    edge_rows = jnp.concatenate([jnp.arange(rows, dtype=jnp.int32), halo_row[None]])
-    away = 1 << 20
-    src_row = jnp.concatenate([own_row, jnp.full((columns,), 1, jnp.int32) * halo_row, edge_rows, edge_rows])
-    src_col = jnp.concatenate(
-        [
-            jnp.where(own_col < columns, own_col, away),
-            jnp.arange(columns, dtype=jnp.int32),
-            jnp.full((rows + 1,), -1, jnp.int32),
-            jnp.full((rows + 1,), columns, jnp.int32),
-        ]
-    )
+    out = jnp.arange(columns * frames, dtype=jnp.int32)
+    out_col, out_frame = out // frames, out % frames
+    every = jnp.arange(frames, dtype=jnp.int32)
+    cols = jnp.arange(columns, dtype=jnp.int32)
+    next_frame = jnp.where(ta == 0, frames, -1)
+    src_col = jnp.concatenate([out_col, 0 * every - 1, 0 * every + columns, cols, jnp.array([-1, columns], jnp.int32)])
+    src_frame = jnp.concatenate([out_frame, every, every, jnp.full((columns + 2,), 1, jnp.int32) * next_frame])
     out_at, src_at = wa * columns + out_col, wa * columns + src_col
-    near = (jnp.abs(out_row[:, None] - src_row[None]) <= 1) & (jnp.abs(out_col[:, None] - src_col[None]) <= 1)
+    near = (jnp.abs(out_frame[:, None] - src_frame[None]) <= 1) & (jnp.abs(out_col[:, None] - src_col[None]) <= 1)
     inside = (src_at >= 0) & (src_at < grid_wide)
     same = clip_of(out_at)[:, None] == clip_of(src_at)[None]
-    weights = near & inside[None] & same & (out_col < columns)[:, None]
-    return weights.astype(jnp.bfloat16)
-
-
-def fused_kernel(
-    frames, columns, flags, own, frame, halo, feats, pool, inverse, head, grad_out, head_grad, loss, sums, slopes, feat_keep
-):
-    batch_at, step = pl.program_id(0), pl.program_id(1)
-    _, _, rows, wide, width = feats.shape
-    tokens = rows * wide
+    return (near & inside[None] & same).astype(jnp.bfloat16)
+
+
+def fused_kernel(rows, flags, own, halo_row, halo, feats, pool, inverse, head, grad_out, head_grad, loss, sums, slopes, feat_keep):
+    step = pl.program_id(0)
+    batch, _, columns, frames, width = feats.shape
+    per_batch = columns * frames
+    tokens = batch * per_batch
     classes = head.shape[1]
 
-    def planar(cells_ref_value, halo_value):
-        keep = lax.broadcasted_iota(jnp.int32, cells_ref_value.shape, 1) < columns
-        cells = jnp.where(keep, cells_ref_value, jnp.zeros_like(cells_ref_value)).reshape(tokens, classes)
-        part = jnp.dot(pool[:, :tokens], cells, preferred_element_type=jnp.float32)
-        return part + jnp.dot(pool[:, tokens:], halo_value, preferred_element_type=jnp.float32)
-
-    @pl.when((step == 0) & (batch_at == 0))
+    def planar(slot, cells_of, scale=None):
+        for b in range(batch):
+            cells = jnp.concatenate([cells_of(b).reshape(per_batch, classes), halo[b, 0]], axis=0)
+            part = jnp.dot(pool[...], cells, preferred_element_type=jnp.float32)
+            sums[slot, b * per_batch : (b + 1) * per_batch] = part if scale is None else part * scale
+
+    @pl.when(step == 0)
     def _():
         loss[...] = jnp.zeros_like(loss)
-
-    @pl.when(step == 0)
-    def _():
-        sums[2] = planar(frame[0], halo[0, frames]) * flags[0]
-
-    @pl.when(step < frames)
-    def _():
-        sums[lax.rem(step, 3)] = planar(own[0, 0], halo[0, step])
-
-    @pl.when(step == frames)
-    def _():
-        sums[frames % 3] = planar(frame[0], halo[0, frames]) * flags[1]
-
-    @pl.when(step > 0)
-    def _():
-        at = step - 1
-        keep = lax.broadcasted_iota(jnp.int32, (rows, wide, width), 1) < columns
-        features = jnp.where(keep, feats[0, 0], jnp.zeros((rows, wide, width), feats.dtype)).reshape(tokens, width)
+        planar(rows % 3, lambda b: halo_row[b, 0], flags[0])
+
+    @pl.when((step > 0) & (step <= rows))
+    def _():
+        planar(lax.rem(step - 1, 3), lambda b: own[b, 0])
+
+    @pl.when(step == rows + 1)
+    def _():
+        planar(rows % 3, lambda b: halo_row[b, 0], flags[1])
+
+    @pl.when(step > 1)
+    def _():
+        at = step - 2
+        features = feats[...].reshape(tokens, width)
         student = jnp.dot(features, head[...], preferred_element_type=jnp.float32)
         pooled = (sums[0] + sums[1] + sums[2]) * inverse[0]
         teach = (pooled - jnp.max(pooled, -1, keepdims=True)) * EXP2_SCALE
@@ -119,18 +103,16 @@
         learn_sum = jnp.sum(learn_exp, -1, keepdims=True)
         cross = jnp.sum(teach_exp * (teach - learn), -1, keepdims=True)
         kl = math.log(2.0) * cross / teach_sum + jnp.log(learn_sum) - jnp.log(teach_sum)
-        valid = lax.rem(lax.broadcasted_iota(jnp.int32, (tokens, 1), 0), wide) < columns
-        kl = jnp.sum(jnp.where(valid, kl, 0.0), axis=0, keepdims=True)
-        loss[...] += sharpness_divisor * sharpness_divisor * kl
+        loss[...] += sharpness_divisor * sharpness_divisor * jnp.sum(kl, axis=0, keepdims=True)
         slope = learn_exp * (sharpness_divisor / learn_sum) - teach_exp * (sharpness_divisor / teach_sum)
         slope = slope.astype(jnp.bfloat16)
         grad = lax.dot_general(slope, head[...], (((1,), (1,)), ((), ())), preferred_element_type=jnp.float32)
-        grad_out[0, 0] = grad.astype(grad_out.dtype).reshape(rows, wide, width)
-        where = pl.ds(pl.multiple_of((batch_at * frames + at) * tokens, 16), tokens)
+        grad_out[...] = grad.astype(grad_out.dtype).reshape(grad_out.shape)
+        where = pl.ds(pl.multiple_of(at * tokens, 16), tokens)
         slopes[where] = slope
         feat_keep[where] = features
 
-    @pl.when((step == frames) & (batch_at == pl.num_programs(0) - 1))
+    @pl.when(step == rows + 1)
     def _():
         chunk = 256
 
@@ -260,17 +242,17 @@
 
 
 def local(features, teacher, head_weight):
-    batch, frames, rows, columns, width = features.shape
+    features, teacher = (jnp.transpose(array, (0, 2, 3, 1, 4)) for array in (features, teacher))
+    batch, rows, columns, frames, width = features.shape
     classes = teacher.shape[-1]
-    wide = round_up(columns, 16)
-    tokens = rows * wide
+    per_batch = columns * frames
+    tokens = batch * per_batch
     ta, ha, wa = (lax.axis_index(axis) for axis in AXES)
-    frame, row, left, right = exchange_halo(teacher)
-    halo = jnp.concatenate([row, left, right], axis=2)
-    pool = pool_weights(rows, columns, wide)
+    row, halo = exchange_halo(teacher)
+    pool = pool_weights(columns, frames)
     frame_at = ta * frames + jnp.arange(frames, dtype=jnp.int32)
     row_at = ha * rows + jnp.arange(rows, dtype=jnp.int32)
-    column_at = wa * columns + jnp.arange(wide, dtype=jnp.int32)
+    column_at = wa * columns + jnp.arange(columns, dtype=jnp.int32)
 
     def edge_count(position, length):
         return 3.0 - (position == 0).astype(jnp.float32) - (position == length - 1).astype(jnp.float32)
@@ -279,30 +261,30 @@
     left_ok = (column_at > 0) & (clip_of(column_at - 1) == own_clip)
     right_ok = (column_at < columns * lax.axis_size("wa") - 1) & (clip_of(column_at + 1) == own_clip)
     counts = (
-        edge_count(frame_at, frames * lax.axis_size("ta"))[:, None, None]
-        * edge_count(row_at, rows * lax.axis_size("ha"))[None, :, None]
-        * (1.0 + left_ok.astype(jnp.float32) + right_ok.astype(jnp.float32))[None, None]
+        edge_count(row_at, rows * lax.axis_size("ha"))[:, None, None, None]
+        * (1.0 + left_ok.astype(jnp.float32) + right_ok.astype(jnp.float32))[None, None, :, None]
+        * edge_count(frame_at, frames * lax.axis_size("ta"))[None, None, None]
     )
-    inverse = (1.0 / counts).reshape(frames, tokens, 1)
-    flags = jnp.stack([(ta == 1), (ta == 0)]).astype(jnp.float32)
+    inverse = jnp.broadcast_to(1.0 / counts, (rows, batch, columns, frames)).reshape(rows, tokens, 1)
+    flags = jnp.stack([(ha == 1), (ha == 0)]).astype(jnp.float32)
     head_bf = head_weight.astype(jnp.bfloat16)
-    lag = lambda b, i: (b, jnp.maximum(i - 1, 0), 0, 0, 0)
-    whole = lambda b, i: (0, 0)
+    lag = lambda i: (0, jnp.maximum(i - 2, 0), 0, 0, 0)
+    whole = lambda i: (0, 0)
     feature_grad, local_grad, loss = pl.pallas_call(
-        functools.partial(fused_kernel, frames, columns),
-        grid=(batch, frames + 1),
+        functools.partial(fused_kernel, rows),
+        grid=(rows + 2,),
         in_specs=[
             pl.BlockSpec(memory_space=pltpu.SMEM),
-            pl.BlockSpec((1, 1, rows, wide, classes), lambda b, i: (b, jnp.minimum(i, frames - 1), 0, 0, 0)),
-            pl.BlockSpec((1, rows, wide, classes), lambda b, i: (b, 0, 0, 0)),
-            pl.BlockSpec((1,) + halo.shape[1:], lambda b, i: (b, 0, 0, 0)),
-            pl.BlockSpec((1, 1, rows, wide, width), lag),
+            pl.BlockSpec((batch, 1, columns, frames, classes), lambda i: (0, jnp.clip(i - 1, 0, rows - 1), 0, 0, 0)),
+            pl.BlockSpec(row.shape, lambda i: (0, 0, 0, 0, 0)),
+            pl.BlockSpec((batch, 1) + halo.shape[2:], lambda i: (0, jnp.where(i == 0, rows, i - 1), 0, 0)),
+            pl.BlockSpec((batch, 1, columns, frames, width), lag),
             pl.BlockSpec(pool.shape, whole),
-            pl.BlockSpec((1, tokens, 1), lambda b, i: (jnp.maximum(i - 1, 0), 0, 0)),
+            pl.BlockSpec((1, tokens, 1), lambda i: (jnp.maximum(i - 2, 0), 0, 0)),
             pl.BlockSpec(head_bf.shape, whole),
         ],
         out_specs=[
-            pl.BlockSpec((1, 1, rows, wide, width), lag),
+            pl.BlockSpec((batch, 1, columns, frames, width), lag),
             pl.BlockSpec((width, classes), whole),
             pl.BlockSpec((1, 1), whole),
         ],
@@ -313,11 +295,12 @@
         ],
         scratch_shapes=[
             pltpu.VMEM((3, tokens, classes), jnp.float32),
-            pltpu.VMEM((batch * frames * tokens, classes), jnp.bfloat16),
-            pltpu.VMEM((batch * frames * tokens, width), jnp.bfloat16),
+            pltpu.VMEM((rows * tokens, classes), jnp.bfloat16),
+            pltpu.VMEM((rows * tokens, width), jnp.bfloat16),
         ],
         compiler_params=pltpu.CompilerParams(vmem_limit_bytes=60 * 1024 * 1024),
-    )(flags, teacher, frame, halo, features, pool, inverse, head_bf)
+    )(flags, teacher, row, halo, features, pool, inverse, head_bf)
+    feature_grad = jnp.transpose(feature_grad, (0, 3, 1, 2, 4))
     owned = width // lax.axis_size(AXES)
     weight_rows = lax.dynamic_slice_in_dim(head_weight, lax.axis_index(AXES) * owned, owned, 0)
     new_weight, loss = reduce_and_update(local_grad, loss, weight_rows)

time: 188 us -> 156 us (0.83)
  local copies, waits for them, and re-layouts: 53.1 us -> 28.3 us
  Pallas kernels: 95.4 us -> 86.1 us
  waiting for transfers between devices: 11.3 us -> 19.1 us
  other arithmetic: 16.2 us -> 11.6 us
    unnamed x27 -> x7, local copies, waits for them, and re-layouts: 32.3 us -> 5.94 us
    slice x4 -> x0, local copies, waits for them, and re-layouts: 10.6 us -> none  [the longest x1 8.07 us: exchange_halo(): frame = jnp.where(ta == 0, teacher[:, -1], teacher[:, 0])]
    concatenate x1 -> x2, local copies, waits for them, and re-layouts: 0.08 us -> 9.19 us  [the longest x1 9.11 us: exchange_halo(): jnp.concatenate([left, right, frame, frame_left, frame_right], 2)]
    pallas_call x1, Pallas kernels: 53.1 us -> 44.1 us  [local(): pl.pallas_call(functools.partial(fused_kernel, rows), grid=(rows + 2,), i...]
    ppermute x4 -> x5, waiting for transfers between devices: 11.3 us -> 19.1 us  [the longest x1 19 us: exchange_halo(): lax.ppermute(jnp.concatenate([teacher[:, :, -1], row[:, :, -1]], 1), 'wa'...]
    reduce_sum x0 -> x3, other arithmetic: none -> 7.05 us  [facing_frame(): return jnp.sum(jnp.where(facing, cells, jnp.zeros_like(cells)), axis=-2)]
    concatenate x5, other arithmetic: 5.99 us -> 0.38 us  [the longest x1 0.14 us: exchange_halo(): frame = jnp.concatenate([frame, edges[:, None, :columns]], 1)]
    select_n x5 -> x1, other arithmetic: 4.8 us -> 0.01 us  [pool_weights(): out_col, out_frame = (out // frames, out % frames)]
  transfers between devices with their start and end apart: 4 -> 5, of which waited for: 1 -> 1; matrix products, arithmetic and copies ran while one was open for 22% -> 17% of each run, Pallas kernels for 0% -> 0%
where the time goes in v3:
time: 156 us
  Pallas kernels  86.1 us (55%)
  local copies, waits for them, and re-layouts  28.3 us (18%)
  waiting for transfers between devices  19.1 us (12%)
  other arithmetic  11.6 us (7%)
  starting transfers between devices  8.04 us (5%)
  between operations  2.63 us (2%)
    pallas_call x1, Pallas kernels, local(): pl.pallas_call(functools.partial(fused_kernel, rows), grid=(rows + 2,), i...  44.1 us
    pallas_call x1, Pallas kernels, reduce_and_update(): pl.pallas_call(functools.partial(reduce_kernel, peers), in_specs=[vmem] *...  42 us
    ppermute x1, waiting for transfers between devices, exchange_halo(): lax.ppermute(jnp.concatenate([teacher[:, :, -1], row[:, :, -1]], 1), 'wa'...  19 us
    concatenate x1, local copies, waits for them, and re-layouts, exchange_halo(): jnp.concatenate([left, right, frame, frame_left, frame_right], 2)  9.11 us
    reduce_sum x3, other arithmetic, facing_frame(): return jnp.sum(jnp.where(facing, cells, jnp.zeros_like(cells)), axis=-2)  7.05 us
    unnamed x7, local copies, waits for them, and re-layouts  5.94 us
    ppermute x1, starting transfers between devices, exchange_halo(): lax.ppermute(jnp.concatenate([teacher[:, :, -1], row[:, :, -1]], 1), 'wa'...  3.45 us
  transfers between devices with their start and end apart: 5, of which 1 were waited for; matrix products, arithmetic and copies ran while one was open for 17% of the time, Pallas kernels for 0%

profile of v3, /device:TPU:0, one launch (start us, length us, event | category | flops | bytes accessed | tf_op | source)
XLA Modules:
  0.0 155.7 jit_solution(13392463387174555803)
XLA Ops:
  0.6 1.9 %copy_bitcast_fusion.1 = bf16[2,1,14,8,1000]{4,3,0,2,1:T(8,128)(2,1)} fusion(bf16[2,8,14,14,1000]{4,1,3,2,0:T(8,128)(2,1)} %param.5, s32[]{:T(128)S(6)} %select_n.102), kind=kLoop, calls=%fused_computation.9 | loop fusion | bytes 906756 | tf_op jit(solution)/shard_map/dynamic_slice | solution.py:37
  2.5 3.0 %collective-permute-start = (bf16[2,1,14,8,1000]{4,3,0,2,1:T(8,128)(2,1)}, bf16[2,1,14,8,1000]{4,3,0,2,1:T(8,128)(2,1)S(1)}, u32[]{:S(2)}, u32[]{:S(2)}) collective-permute-start(bf16[2,1,14,8,1000]{4,3,0,2,1:T(8,128)(2,1)} %copy_bitcast_fusion.1), channel_id=1, source_target_pairs={{0,8},{8,0},{1,9},{9,1},{2,10},{10,2},{3,11},{11,3},{4,12},{12,4},... | collective-permute-start | bytes 1344008 | tf_op jit(solution)/shard_map/ppermute | solution.py:38
  5.5 0.0 copy-start
  5.5 6.2 %select_reduce_fusion = bf16[2,14,14,1000]{3,1,0,2:T(8,128)(2,1)S(1)} fusion(pred[8]{0:T(512)(128)(4,1)S(1)} %iota_compare_fusion, bf16[2,8,14,14,1000]{4,1,3,2,0:T(8,128)(2,1)} %param.5), kind=kLoop, calls=%fused_computation.1 | loop fusion | flops 5880000 | bytes 7056008 | tf_op jit(solution)/shard_map/reduce_sum | solution.py:35
  11.6 0.8 copy.57
  12.5 0.1 collective-permute-start.3
  12.6 0.0 copy-done
  12.6 3.5 %copy.82 = bf16[2,8,14,14,1000]{4,1,2,0,3:T(8,128)(2,1)} copy(bf16[2,8,14,14,1000]{4,1,3,2,0:T(8,128)(2,1)S(1)} %copy-done) | data formatting | bytes 12544000 | tf_op args[1]
  16.2 0.1 broadcast_multiply_fusion
  16.2 0.1 multiply_divide_fusion
  16.4 3.0 %copy.67.inverse = f32[14,224,1]{2,1,0:T(8,128)} copy(f32[14,224,1]{0,1,2:T(8,128)S(1)} %bitcast.39) | data formatting | bytes 25088 | tf_op jit(solution)/shard_map/reshape | solution.py:268
  19.4 0.0 copy-start.1
  19.4 2.5 %convert_element_type.67 = bf16[1024,1000]{0,1:T(8,128)(2,1)S(1)} convert(f32[1024,1000]{0,1:T(8,128)} %param.6) | non-fusion elementwise | flops 1024000 | bytes 6144000 | tf_op jit(solution)/shard_map/convert_element_type | solution.py:270
  21.8 2.6 %copy.68.head = bf16[1024,1000]{1,0:T(8,128)(2,1)} copy(bf16[1024,1000]{0,1:T(8,128)(2,1)S(1)} %convert_element_type.67) | data formatting | bytes 4096000 | tf_op jit(solution)/shard_map/convert_element_type | solution.py:270
  24.4 1.2 constant_dynamic-slice_fusion
  25.6 0.8 copy.76.weight
  26.5 0.1 pad_add_fusion
  26.6 0.0 copy-done.1
  26.6 0.1 concatenate.34
  26.7 1.2 slice_bitcast_fusion
  27.9 0.0 collective-permute-done
  27.9 0.1 pad_maximum_fusion.1
  28.0 3.5 %collective-permute-start.1 = (bf16[2,15,8,1000]{3,2,1,0:T(8,128)(2,1)S(1)}, bf16[2,15,8,1000]{3,2,1,0:T(8,128)(2,1)S(1)}, u32[]{:S(2)}, u32[]{:S(2)}) collective-permute-start(bf16[2,15,8,1000]{3,2,1,0:T(8,128)(2,1)S(1)} %pad_maximum_fusion.1), channel_id=1, source_target_pairs={{0,1},{1,2},{2,3},{3,4},{4,5},{5,6},{6,7},{8,9},{9,10},{10,11},{11... | collective-permute-start | bytes 1440008 | tf_op jit(solution)/shard_map/ppermute | solution.py:40
  31.5 0.1 pad_maximum_fusion.2
  31.5 1.5 collective-permute-start.2
  33.0 0.7 add_convert_fusion.flags
  33.7 0.3 fusion
  34.0 19.0 %collective-permute-done.1 = bf16[2,15,8,1000]{3,2,1,0:T(8,128)(2,1)S(1)} collective-permute-done((bf16[2,15,8,1000]{3,2,1,0:T(8,128)(2,1)S(1)}, bf16[2,15,8,1000]{3,2,1,0:T(8,128)(2,1)S(1)}, u32[]{:S(2)}, u32[]{:S(2)}) %collective-permute-start.1) | collective-permute-done | bytes 480032 | tf_op jit(solution)/shard_map/ppermute | solution.py:40
  53.1 0.0 collective-permute-done.2
  53.1 0.5 select_reduce_fusion.2
  53.6 0.1 pad_maximum_fusion.3
  53.7 0.1 collective-permute-start.4
  53.8 0.8 fusion.4.pool
  54.5 0.8 copy.66.halo_row
  55.3 0.0 collective-permute-done.3
  55.4 1.4 copy.59
  56.7 0.0 collective-permute-done.4
  56.8 0.1 copy.62
  56.9 0.1 copy.63
  57.0 0.1 pad_maximum_fusion
  57.1 9.1 %concatenate.32.halo = bf16[2,15,32,1000]{3,2,1,0:T(8,128)(2,1)} concatenate(bf16[2,15,8,1000]{3,2,1,0:T(8,128)(2,1)S(1)} %collective-permute-done.1, bf16[2,15,8,1000]{3,2,1,0:T(8,128)(2,1)S(1)} %collective-permute-done.2, bf16[2,15,14,1000]{3,2,1,0:T(8,128)(2,1)S(1)} %pad_maximum_fusion, bf16[2,15,1,1000]{3,2,1,0:T(2,128)(2,1)S(1)} %copy.62, bf16[2,15,1,1000]{3,2,1,0:T(2,128)(2,1)S(1)} %copy.63), dimensions={2} | concatenate | bytes 3840000 | tf_op jit(solution)/shard_map/concatenate | solution.py:47
  66.3 44.1 %shard_map.67 = (bf16[2,14,14,8,1024]{4,3,2,1,0:T(8,128)(2,1)}, bf16[1024,1000]{1,0:T(8,128)(2,1)}, f32[1,1]{1,0:T(1,128)}) custom-call(f32[2]{0:T(128)} %add_convert_fusion.flags, bf16[2,14,14,8,1000]{4,3,2,1,0:T(8,128)(2,1)} %bitcast.35, bf16[2,1,14,8,1000]{4,3,2,1,0:T(8,128)(2,1)} %copy.66.halo_row, bf16[2,15,32,1000]{3,2,1,0:T(8,128)(2,1)} %concatenate.32.halo, ...), custom_call_target="tpu_custom_call" | custom-call | tf_op jit(solution)/shard_map/pallas_call | solution.py:273
  110.4 42.0 %shard_map.68 = (f32[32,1000]{1,0:T(8,128)}, f32[1,1]{1,0:T(1,128)}) custom-call(bf16[2,16,32,1000]{3,2,1,0:T(8,128)(2,1)} %bitcast.38, f32[1,1]{1,0:T(1,128)} %get-tuple-element.10.local_loss, f32[32,1000]{1,0:T(8,128)} %copy.76.weight), custom_call_target="tpu_custom_call" | custom-call | tf_op jit(solution)/shard_map/pallas_call | solution.py:227
  153.0 1.6 %copy.86 = f32[32,1000]{1,0:T(8,128)} copy(f32[32,1000]{1,0:T(8,128)} %get-tuple-element.30) | data formatting | bytes 256000
  (17 shorter events, 0.2 us)
Async XLA Ops:
  2.5 25.4 %collective-permute-start = (bf16[2,1,14,8,1000]{4,3,0,2,1:T(8,128)(2,1)}, bf16[2,1,14,8,1000]{4,3,0,2,1:T(8,128)(2,1)S(1)}, u32[]{:S(2)}, u32[]{:S(2)}) collective-permute-start(bf16[2,1,14,8,1000]{4,3,0,2,1:T(8,128)(2,1)} %copy_bitcast_fusion.1), channel_id=1, source_target_pairs={{0,8},{8,0},{1,9},{9,1},{2,10},{10,2},{3,11},{11,3},{4,12},{12,4},... | collective-permute-start | bytes 1344008 | tf_op jit(solution)/shard_map/ppermute | solution.py:38
  5.5 7.1 %copy-start = (bf16[2,8,14,14,1000]{4,1,3,2,0:T(8,128)(2,1)S(1)}, bf16[2,8,14,14,1000]{4,1,3,2,0:T(8,128)(2,1)}, u32[]{:S(2)}) copy-start(bf16[2,8,14,14,1000]{4,1,3,2,0:T(8,128)(2,1)} %param.5) | copy-start | bytes 18816004
  12.5 42.9 %collective-permute-start.3 = (bf16[2,14,14,1000]{3,0,2,1:T(2,128)(2,1)S(1)}, bf16[2,14,14,1000]{3,0,2,1:T(2,128)(2,1)}, u32[]{:S(2)}, u32[]{:S(2)}) collective-permute-start(bf16[2,14,14,1000]{3,0,2,1:T(2,128)(2,1)S(1)} %copy.57), channel_id=1, source_target_pairs={{0,16},{16,0},{1,17},{17,1},{2,18},{18,2},{3,19},{19,3},{4,20},{20... | collective-permute-start | bytes 2352008 | tf_op jit(solution)/shard_map/ppermute | solution.py:39
  19.4 7.2 %copy-start.1 = (s32[2]{0:T(128)S(1)}, s32[2]{0:T(128)}, u32[]{:S(2)}) copy-start(s32[2]{0:T(128)} %constant.142.clone) | copy-start | bytes 28
  28.0 25.1 %collective-permute-start.1 = (bf16[2,15,8,1000]{3,2,1,0:T(8,128)(2,1)S(1)}, bf16[2,15,8,1000]{3,2,1,0:T(8,128)(2,1)S(1)}, u32[]{:S(2)}, u32[]{:S(2)}) collective-permute-start(bf16[2,15,8,1000]{3,2,1,0:T(8,128)(2,1)S(1)} %pad_maximum_fusion.1), channel_id=1, source_target_pairs={{0,1},{1,2},{2,3},{3,4},{4,5},{5,6},{6,7},{8,9},{9,10},{10,11},{11... | collective-permute-start | bytes 1440008 | tf_op jit(solution)/shard_map/ppermute | solution.py:40
  31.5 21.6 %collective-permute-start.2 = (bf16[2,15,8,1000]{3,2,1,0:T(8,128)(2,1)S(1)}, bf16[2,15,8,1000]{3,2,1,0:T(8,128)(2,1)S(1)}, u32[]{:S(2)}, u32[]{:S(2)}) collective-permute-start(bf16[2,15,8,1000]{3,2,1,0:T(8,128)(2,1)S(1)} %pad_maximum_fusion.2), channel_id=1, source_target_pairs={{1,0},{2,1},{3,2},{4,3},{5,4},{6,5},{7,6},{9,8},{10,9},{11,10},{12... | collective-permute-start | bytes 1440008 | tf_op jit(solution)/shard_map/ppermute | solution.py:41
  53.7 3.0 %collective-permute-start.4 = (bf16[2,44,1000]{2,1,0:T(8,128)(2,1)S(1)}, bf16[2,44,1000]{2,1,0:T(8,128)(2,1)S(1)}, u32[]{:S(2)}, u32[]{:S(2)}) collective-permute-start(bf16[2,44,1000]{2,1,0:T(8,128)(2,1)S(1)} %pad_maximum_fusion.3), channel_id=1, source_target_pairs={{0,16},{16,0},{1,17},{17,1},{2,18},{18,2},{3,19},{19,3},{4,20},{20... | collective-permute-start | bytes 528008 | tf_op jit(solution)/shard_map/ppermute | solution.py:43

commit v4 on v3

--- a/solution.py
+++ b/solution.py
@@ -34,17 +34,25 @@
         facing = lax.broadcasted_iota(jnp.int32, cells.shape, cells.ndim - 2) == jnp.where(ta == 0, frames - 1, 0)
         return jnp.sum(jnp.where(facing, cells, jnp.zeros_like(cells)), axis=-2)
 
-    row = lax.dynamic_slice_in_dim(teacher, jnp.where(ha == 0, rows - 1, 0), 1, 1)
-    row = lax.ppermute(row, "ha", swap)
+    wa = lax.axis_index("wa")
+    facing_row = jnp.where(ha == 0, rows - 1, 0)
+
+    def column(at):
+        return lax.dynamic_slice_in_dim(teacher, at, 1, 2)[:, :, 0]
+
+    left = lax.ppermute(column(jnp.minimum(wa + columns - 1, columns - 1)), "wa", forward)
+    right = lax.ppermute(column(jnp.maximum(-wa, 0)), "wa", backward)
+    row = lax.ppermute(lax.dynamic_slice_in_dim(teacher, facing_row, 1, 1), "ha", swap)
     frame = lax.ppermute(facing_frame(teacher), "ta", swap)
-    left = lax.ppermute(jnp.concatenate([teacher[:, :, -1], row[:, :, -1]], 1), "wa", forward)
-    right = lax.ppermute(jnp.concatenate([teacher[:, :, 0], row[:, :, 0]], 1), "wa", backward)
-    edges = jnp.concatenate([facing_frame(row[:, 0]), facing_frame(left), facing_frame(right)], 1)
-    edges = lax.ppermute(edges, "ta", swap)
+    sides = jnp.concatenate([left, right], 2)
+    corner = lax.ppermute(lax.dynamic_slice_in_dim(sides, facing_row, 1, 1), "ha", swap)
+    sides = jnp.concatenate([sides, corner], 1)
+    edges = [facing_frame(part) for part in (row[:, 0], sides[:, :, :frames], sides[:, :, frames:])]
+    edges = lax.ppermute(jnp.concatenate(edges, 1), "ta", swap)
     frame = jnp.concatenate([frame, edges[:, None, :columns]], 1)
     frame_left = edges[:, columns : columns + rows + 1, None]
     frame_right = edges[:, columns + rows + 1 :, None]
-    return row, jnp.concatenate([left, right, frame, frame_left, frame_right], 2)
+    return row, sides, jnp.concatenate([frame, frame_left, frame_right], 2)
 
 
 def pool_weights(columns, frames):
@@ -64,7 +72,7 @@
     return (near & inside[None] & same).astype(jnp.bfloat16)
 
 
-def fused_kernel(rows, flags, own, halo_row, halo, feats, pool, inverse, head, grad_out, head_grad, loss, sums, slopes, feat_keep):
+def fused_kernel(rows, flags, own, halo_row, sides, ahead, feats, pool, inverse, head, grad_out, head_grad, loss, sums, slopes, feat_keep):
     step = pl.program_id(0)
     batch, _, columns, frames, width = feats.shape
     per_batch = columns * frames
@@ -73,7 +81,7 @@
 
     def planar(slot, cells_of, scale=None):
         for b in range(batch):
-            cells = jnp.concatenate([cells_of(b).reshape(per_batch, classes), halo[b, 0]], axis=0)
+            cells = jnp.concatenate([cells_of(b).reshape(per_batch, classes), sides[b, 0], ahead[b, 0]], axis=0)
             part = jnp.dot(pool[...], cells, preferred_element_type=jnp.float32)
             sums[slot, b * per_batch : (b + 1) * per_batch] = part if scale is None else part * scale
 
@@ -248,7 +256,7 @@
     per_batch = columns * frames
     tokens = batch * per_batch
     ta, ha, wa = (lax.axis_index(axis) for axis in AXES)
-    row, halo = exchange_halo(teacher)
+    row, sides, ahead = exchange_halo(teacher)
     pool = pool_weights(columns, frames)
     frame_at = ta * frames + jnp.arange(frames, dtype=jnp.int32)
     row_at = ha * rows + jnp.arange(rows, dtype=jnp.int32)
@@ -269,6 +277,7 @@
     flags = jnp.stack([(ha == 1), (ha == 0)]).astype(jnp.float32)
     head_bf = head_weight.astype(jnp.bfloat16)
     lag = lambda i: (0, jnp.maximum(i - 2, 0), 0, 0, 0)
+    beside = lambda i: (0, jnp.where(i == 0, rows, i - 1), 0, 0)
     whole = lambda i: (0, 0)
     feature_grad, local_grad, loss = pl.pallas_call(
         functools.partial(fused_kernel, rows),
@@ -277,7 +286,8 @@
             pl.BlockSpec(memory_space=pltpu.SMEM),
             pl.BlockSpec((batch, 1, columns, frames, classes), lambda i: (0, jnp.clip(i - 1, 0, rows - 1), 0, 0, 0)),
             pl.BlockSpec(row.shape, lambda i: (0, 0, 0, 0, 0)),
-            pl.BlockSpec((batch, 1) + halo.shape[2:], lambda i: (0, jnp.where(i == 0, rows, i - 1), 0, 0)),
+            pl.BlockSpec((batch, 1) + sides.shape[2:], beside),
+            pl.BlockSpec((batch, 1) + ahead.shape[2:], beside),
             pl.BlockSpec((batch, 1, columns, frames, width), lag),
             pl.BlockSpec(pool.shape, whole),
             pl.BlockSpec((1, tokens, 1), lambda i: (jnp.maximum(i - 2, 0), 0, 0)),
@@ -299,7 +309,7 @@
             pltpu.VMEM((rows * tokens, width), jnp.bfloat16),
         ],
         compiler_params=pltpu.CompilerParams(vmem_limit_bytes=60 * 1024 * 1024),
-    )(flags, teacher, row, halo, features, pool, inverse, head_bf)
+    )(flags, teacher, row, sides, ahead, features, pool, inverse, head_bf)
     feature_grad = jnp.transpose(feature_grad, (0, 3, 1, 2, 4))
     owned = width // lax.axis_size(AXES)
     weight_rows = lax.dynamic_slice_in_dim(head_weight, lax.axis_index(AXES) * owned, owned, 0)

time: 156 us -> 138 us (0.88)
  waiting for transfers between devices: 19.1 us -> 6.89 us
  local copies, waits for them, and re-layouts: 28.3 us -> 19.5 us
    ppermute x4 -> x5, waiting for transfers between devices: 19.1 us -> 6.89 us  [the longest x1 4.42 us: exchange_halo(): lax.ppermute(column(jnp.minimum(wa + columns - 1, columns - 1)), 'wa', fo...]
    concatenate x1, local copies, waits for them, and re-layouts: 9.11 us -> 0.03 us  [exchange_halo(): sides = jnp.concatenate([left, right], 2)]
    unnamed x7 -> x11, local copies, waits for them, and re-layouts: 5.94 us -> 2.45 us
    concatenate x5 -> x3, other arithmetic: 0.38 us -> 3.28 us  [the longest x1 1.46 us: exchange_halo(): return (row, sides, jnp.concatenate([frame, frame_left, frame_right], 2))]
    convert_element_type x1, other arithmetic: 2.49 us -> 0.31 us  [local(): head_bf = head_weight.astype(jnp.bfloat16)]
    ppermute x4 -> x5, starting transfers between devices: 7.96 us -> 9.32 us  [the longest x1 4.92 us: exchange_halo(): lax.ppermute(column(jnp.minimum(wa + columns - 1, columns - 1)), 'wa', fo...]
  transfers between devices with their start and end apart: 5 -> 6, of which waited for: 1 -> 2; matrix products, arithmetic and copies ran while one was open for 17% -> 19% of each run, Pallas kernels for 0% -> 0%
where the time goes in v4:
time: 138 us
  Pallas kernels  86.7 us (63%)
  local copies, waits for them, and re-layouts  19.5 us (14%)
  other arithmetic  12.8 us (9%)
  starting transfers between devices  9.33 us (7%)
  waiting for transfers between devices  6.89 us (5%)
  between operations  2.6 us (2%)
    pallas_call x1, Pallas kernels, local(): pl.pallas_call(functools.partial(fused_kernel, rows), grid=(rows + 2,), i...  44.2 us
    pallas_call x1, Pallas kernels, reduce_and_update(): pl.pallas_call(functools.partial(reduce_kernel, peers), in_specs=[vmem] *...  42.5 us
    reduce_sum x3, other arithmetic, facing_frame(): return jnp.sum(jnp.where(facing, cells, jnp.zeros_like(cells)), axis=-2)  6.87 us
    ppermute x1, starting transfers between devices, exchange_halo(): lax.ppermute(column(jnp.minimum(wa + columns - 1, columns - 1)), 'wa', fo...  4.92 us
    ppermute x1, waiting for transfers between devices, exchange_halo(): lax.ppermute(column(jnp.minimum(wa + columns - 1, columns - 1)), 'wa', fo...  4.42 us
    reshape x1, local copies, waits for them, and re-layouts, local(): jnp.broadcast_to(1.0 / counts, (rows, batch, columns, frames))  3.91 us
  transfers between devices with their start and end apart: 6, of which 2 were waited for; matrix products, arithmetic and copies ran while one was open for 19% of the time, Pallas kernels for 0%

profile of v4, /device:TPU:0, one launch (start us, length us, event | category | flops | bytes accessed | tf_op | source)
XLA Modules:
  0.0 137.8 jit_solution(2374346218263737869)
XLA Ops:
  0.6 2.0 %dynamic-slice_bitcast_fusion = (bf16[2,14,8,1000]{3,2,1,0:T(8,128)(2,1)}, bf16[2,14,8,1000]{3,2,1,0:T(8,128)(2,1)S(1)}) fusion(bf16[2,8,14,14,1000]{4,1,3,2,0:T(8,128)(2,1)} %param.5, s32[]{:T(128)S(6)} %max.3, s32[]{:T(128)S(6)} %select_n.108), kind=kLoop, calls=%fused_computation.15 | loop fusion | bytes 1792008 | tf_op jit(solution)/shard_map/squeeze | solution.py:41
  2.6 4.9 %collective-permute-start.1 = (bf16[2,14,8,1000]{3,2,1,0:T(8,128)(2,1)S(1)}, bf16[2,14,8,1000]{3,2,1,0:T(8,128)(2,1)S(1)}, u32[]{:S(2)}, u32[]{:S(2)}) collective-permute-start(bf16[2,14,8,1000]{3,2,1,0:T(8,128)(2,1)S(1)} %get-tuple-element.16), channel_id=1, source_target_pairs={{0,1},{1,2},{2,3},{3,4},{4,5},{5,6},{6,7},{8,9},{9,10},{10,11},{11... | collective-permute-start | bytes 1344008 | tf_op jit(solution)/shard_map/ppermute | solution.py:43
  7.6 1.3 collective-permute-start.2
  8.9 1.1 dynamic-slice_bitcast_fusion.2
  9.9 1.6 %collective-permute-start = (bf16[2,1,14,8,1000]{4,3,2,1,0:T(8,128)(2,1)S(1)}, bf16[2,1,14,8,1000]{4,3,2,1,0:T(8,128)(2,1)S(1)}, u32[]{:S(2)}, u32[]{:S(2)}) collective-permute-start(bf16[2,1,14,8,1000]{4,3,2,1,0:T(8,128)(2,1)S(1)} %dynamic-slice_bitcast_fusion.2), channel_id=1, source_target_pairs={{0,8},{8,0},{1,9},{9,1},{2,10},{10,2},{3,11},{11,3},{4,12},{12,4},... | collective-permute-start | bytes 1344008 | tf_op jit(solution)/shard_map/ppermute | solution.py:45
  11.5 0.0 copy-start.3
  11.5 6.0 %select_reduce_fusion = bf16[2,14,14,1000]{3,2,1,0:T(8,128)(2,1)S(1)} fusion(pred[8]{0:T(512)(128)(4,1)S(1)} %iota_compare_fusion, bf16[2,8,14,14,1000]{4,1,3,2,0:T(8,128)(2,1)} %param.5), kind=kLoop, calls=%fused_computation | loop fusion | flops 5880000 | bytes 7056008 | tf_op jit(solution)/shard_map/reduce_sum | solution.py:35
  17.5 1.7 %copy.53 = bf16[2,14,14,1000]{3,0,2,1:T(2,128)(2,1)} copy(bf16[2,14,14,1000]{3,2,1,0:T(8,128)(2,1)S(1)} %select_reduce_fusion) | data formatting | bytes 1568000 | tf_op jit(solution)/shard_map/reduce_sum | solution.py:35
  19.2 0.0 collective-permute-start.4
  19.3 0.0 copy-done.3
  19.3 0.1 concatenate.34
  19.4 0.1 broadcast_multiply_fusion
  19.5 0.7 multiply_divide_fusion
  20.2 0.0 copy-start
  20.2 0.1 and_select_fusion.3
  20.3 0.8 fusion.10.pool
  21.1 1.6 %constant_dynamic-slice_fusion = f32[32,1000]{0,1:T(8,128)S(1)} fusion(f32[1024,1000]{0,1:T(8,128)} %param.6, s32[]{:T(128)S(6)} %select_n.122), kind=kLoop, calls=%fused_computation.47 | loop fusion | bytes 256004 | tf_op jit(solution)/shard_map/dynamic_slice | solution.py:315
  22.7 4.4 %collective-permute-done.1 = bf16[2,14,8,1000]{3,2,1,0:T(8,128)(2,1)S(1)} collective-permute-done((bf16[2,14,8,1000]{3,2,1,0:T(8,128)(2,1)S(1)}, bf16[2,14,8,1000]{3,2,1,0:T(8,128)(2,1)S(1)}, u32[]{:S(2)}, u32[]{:S(2)}) %collective-permute-start.1) | collective-permute-done | bytes 448032 | tf_op jit(solution)/shard_map/ppermute | solution.py:43
  27.2 0.0 collective-permute-done.2
  27.2 1.6 %collective-permute-start.3 = (bf16[2,1,16,1000]{3,2,1,0:T(8,128)(2,1)S(1)}, bf16[2,1,16,1000]{3,2,1,0:T(8,128)(2,1)S(1)}, u32[]{:S(2)}, u32[]{:S(2)}) collective-permute-start(bf16[2,1,16,1000]{3,2,1,0:T(8,128)(2,1)S(1)} %constant_dynamic-slice_fusion.1), channel_id=1, source_target_pairs={{0,8},{8,0},{1,9},{9,1},{2,10},{10,2},{3,11},{11,3},{4,12},{12,4},... | collective-permute-start | bytes 192008 | tf_op jit(solution)/shard_map/ppermute | solution.py:48
  28.8 0.0 collective-permute-done.halo_row
  28.8 0.0 copy-start.1
  28.8 0.3 fusion.6
  29.1 2.5 %collective-permute-done.3 = bf16[2,1,16,1000]{3,2,1,0:T(8,128)(2,1)S(1)} collective-permute-done((bf16[2,1,16,1000]{3,2,1,0:T(8,128)(2,1)S(1)}, bf16[2,1,16,1000]{3,2,1,0:T(8,128)(2,1)S(1)}, u32[]{:S(2)}, u32[]{:S(2)}) %collective-permute-start.3) | collective-permute-done | bytes 64032 | tf_op jit(solution)/shard_map/ppermute | solution.py:48
  31.6 0.5 fusion.5
  32.1 0.0 copy-start.2
  32.1 0.7 pad_maximum_fusion.2
  32.9 0.0 collective-permute-start.5
  32.9 0.0 copy-done.1
  32.9 0.6 add_convert_fusion.flags
  33.5 0.0 copy-done
  33.5 0.3 convert_element_type.67
  33.8 0.0 copy-done.2
  33.9 0.7 broadcast_in_dim.17
  34.5 3.9 %copy.60.inverse = f32[14,224,1]{2,1,0:T(8,128)} copy(f32[14,224,1]{0,1,2:T(8,128)} %bitcast.36) | data formatting | bytes 25088 | tf_op jit(solution)/shard_map/reshape | solution.py:276
  38.4 2.5 %copy.61.head = bf16[1024,1000]{1,0:T(8,128)(2,1)} copy(bf16[1024,1000]{0,1:T(8,128)(2,1)S(1)} %convert_element_type.67) | data formatting | bytes 4096000 | tf_op jit(solution)/shard_map/convert_element_type | solution.py:278
  41.0 0.8 copy.69.weight
  41.8 1.1 pad_maximum_fusion.sides
  42.9 0.0 collective-permute-done.5
  42.9 1.0 slice_bitcast_fusion.1
  43.9 0.1 copy.57
  44.0 0.1 copy.58
  44.1 0.8 slice_bitcast_fusion.2
  44.9 0.0 collective-permute-done.4
  44.9 1.4 copy.54
  46.3 1.5 %pad_maximum_fusion.1.ahead = bf16[2,15,16,1000]{3,2,1,0:T(8,128)(2,1)} fusion(bf16[2,15,1,1000]{3,2,1,0:T(2,128)(2,1)S(1)} %copy.58, bf16[2,15,1,1000]{3,2,1,0:T(2,128)(2,1)S(1)} %copy.57, bf16[2,1,14,1000]{3,2,1,0:T(8,128)(2,1)S(1)} %slice_bitcast_fusion.2, bf16[2,14,14,1000]{3,2,1,0:T(8,128)(2,1)S(1)} %copy.54), kind=kLoop, calls=%fused_computation.4 | loop fusion | flops 3840000 | bytes 1920000 | tf_op jit(solution)/shard_map/concatenate | solution.py:55
  47.8 44.2 %shard_map.67 = (bf16[2,14,14,8,1024]{4,3,2,1,0:T(8,128)(2,1)}, bf16[1024,1000]{1,0:T(8,128)(2,1)}, f32[1,1]{1,0:T(1,128)}) custom-call(f32[2]{0:T(128)} %add_convert_fusion.flags, bf16[2,14,14,8,1000]{4,3,2,1,0:T(8,128)(2,1)} %bitcast.33, bf16[2,1,14,8,1000]{4,3,2,1,0:T(8,128)(2,1)} %copy-done.1, bf16[2,15,16,1000]{3,2,1,0:T(8,128)(2,1)} %pad_maximum_fusion.sides, ...), custom_call_target="tpu_custom_call" | custom-call | tf_op jit(solution)/shard_map/pallas_call | solution.py:282
  92.0 42.5 %shard_map.68 = (f32[32,1000]{1,0:T(8,128)}, f32[1,1]{1,0:T(1,128)}) custom-call(bf16[2,16,32,1000]{3,2,1,0:T(8,128)(2,1)} %bitcast.35, f32[1,1]{1,0:T(1,128)} %get-tuple-element.10.local_loss, f32[32,1000]{1,0:T(8,128)} %copy.69.weight), custom_call_target="tpu_custom_call" | custom-call | tf_op jit(solution)/shard_map/pallas_call | solution.py:235
  135.1 1.6 %copy.75 = f32[32,1000]{1,0:T(8,128)} copy(f32[32,1000]{1,0:T(8,128)} %get-tuple-element.26) | data formatting | bytes 256000
  (16 shorter events, 0.2 us)
Async XLA Ops:
  2.6 24.5 %collective-permute-start.1 = (bf16[2,14,8,1000]{3,2,1,0:T(8,128)(2,1)S(1)}, bf16[2,14,8,1000]{3,2,1,0:T(8,128)(2,1)S(1)}, u32[]{:S(2)}, u32[]{:S(2)}) collective-permute-start(bf16[2,14,8,1000]{3,2,1,0:T(8,128)(2,1)S(1)} %get-tuple-element.16), channel_id=1, source_target_pairs={{0,1},{1,2},{2,3},{3,4},{4,5},{5,6},{6,7},{8,9},{9,10},{10,11},{11... | collective-permute-start | bytes 1344008 | tf_op jit(solution)/shard_map/ppermute | solution.py:43
  7.6 19.6 %collective-permute-start.2 = (bf16[2,14,8,1000]{3,2,1,0:T(8,128)(2,1)}, bf16[2,14,8,1000]{3,2,1,0:T(8,128)(2,1)S(1)}, u32[]{:S(2)}, u32[]{:S(2)}) collective-permute-start(bf16[2,14,8,1000]{3,2,1,0:T(8,128)(2,1)} %get-tuple-element.15), channel_id=1, source_target_pairs={{1,0},{2,1},{3,2},{4,3},{5,4},{6,5},{7,6},{9,8},{10,9},{11,10},{12... | collective-permute-start | bytes 1344008 | tf_op jit(solution)/shard_map/ppermute | solution.py:44
  9.9 18.9 %collective-permute-start = (bf16[2,1,14,8,1000]{4,3,2,1,0:T(8,128)(2,1)S(1)}, bf16[2,1,14,8,1000]{4,3,2,1,0:T(8,128)(2,1)S(1)}, u32[]{:S(2)}, u32[]{:S(2)}) collective-permute-start(bf16[2,1,14,8,1000]{4,3,2,1,0:T(8,128)(2,1)S(1)} %dynamic-slice_bitcast_fusion.2), channel_id=1, source_target_pairs={{0,8},{8,0},{1,9},{9,1},{2,10},{10,2},{3,11},{11,3},{4,12},{12,4},... | collective-permute-start | bytes 1344008 | tf_op jit(solution)/shard_map/ppermute | solution.py:45
  11.5 7.8 %copy-start.3 = (s32[2]{0:T(128)S(1)}, s32[2]{0:T(128)}, u32[]{:S(2)}) copy-start(s32[2]{0:T(128)} %constant.145.clone) | copy-start | bytes 28
  19.2 25.7 %collective-permute-start.4 = (bf16[2,14,14,1000]{3,0,2,1:T(2,128)(2,1)}, bf16[2,14,14,1000]{3,0,2,1:T(2,128)(2,1)}, u32[]{:S(2)}, u32[]{:S(2)}) collective-permute-start(bf16[2,14,14,1000]{3,0,2,1:T(2,128)(2,1)} %copy.53), channel_id=1, source_target_pairs={{0,16},{16,0},{1,17},{17,1},{2,18},{18,2},{3,19},{19,3},{4,20},{20... | collective-permute-start | bytes 2352008 | tf_op jit(solution)/shard_map/ppermute | solution.py:46
  20.2 13.3 %copy-start = (f32[1024,1000]{0,1:T(8,128)S(1)}, f32[1024,1000]{0,1:T(8,128)}, u32[]{:S(2)}) copy-start(f32[1024,1000]{0,1:T(8,128)} %param.6) | copy-start | bytes 12288004
  27.2 4.3 %collective-permute-start.3 = (bf16[2,1,16,1000]{3,2,1,0:T(8,128)(2,1)S(1)}, bf16[2,1,16,1000]{3,2,1,0:T(8,128)(2,1)S(1)}, u32[]{:S(2)}, u32[]{:S(2)}) collective-permute-start(bf16[2,1,16,1000]{3,2,1,0:T(8,128)(2,1)S(1)} %constant_dynamic-slice_fusion.1), channel_id=1, source_target_pairs={{0,8},{8,0},{1,9},{9,1},{2,10},{10,2},{3,11},{11,3},{4,12},{12,4},... | collective-permute-start | bytes 192008 | tf_op jit(solution)/shard_map/ppermute | solution.py:48
  28.8 4.1 %copy-start.1 = (bf16[2,1,14,8,1000]{4,3,2,1,0:T(8,128)(2,1)}, bf16[2,1,14,8,1000]{4,3,2,1,0:T(8,128)(2,1)S(1)}, u32[]{:S(2)}) copy-start(bf16[2,1,14,8,1000]{4,3,2,1,0:T(8,128)(2,1)S(1)} %collective-permute-done.halo_row) | copy-start | bytes 1344004
  32.1 1.7 %copy-start.2 = (f32[14,14,8]{0,2,1:T(8,128)S(1)}, f32[14,14,8]{0,2,1:T(8,128)}, u32[]{:S(2)}) copy-start(f32[14,14,8]{0,2,1:T(8,128)} %multiply_divide_fusion) | copy-start | bytes 18820
  32.9 10.0 %collective-permute-start.5 = (bf16[2,44,1000]{2,1,0:T(8,128)(2,1)}, bf16[2,44,1000]{2,1,0:T(8,128)(2,1)}, u32[]{:S(2)}, u32[]{:S(2)}) collective-permute-start(bf16[2,44,1000]{2,1,0:T(8,128)(2,1)} %pad_maximum_fusion.2), channel_id=1, source_target_pairs={{0,16},{16,0},{1,17},{17,1},{2,18},{18,2},{3,19},{19,3},{4,20},{20... | collective-permute-start | bytes 528008 | tf_op jit(solution)/shard_map/ppermute | solution.py:51

commit v5 on v4

--- a/solution.py
+++ b/solution.py
@@ -103,7 +103,7 @@
         at = step - 2
         features = feats[...].reshape(tokens, width)
         student = jnp.dot(features, head[...], preferred_element_type=jnp.float32)
-        pooled = (sums[0] + sums[1] + sums[2]) * inverse[0]
+        pooled = (sums[0] + sums[1] + sums[2]) * (inverse[...] * flags[2 + at])
         teach = (pooled - jnp.max(pooled, -1, keepdims=True)) * EXP2_SCALE
         learn = (student - jnp.max(student, -1, keepdims=True)) * EXP2_SCALE
         teach_exp, learn_exp = jnp.exp2(teach), jnp.exp2(learn)
@@ -269,12 +269,12 @@
     left_ok = (column_at > 0) & (clip_of(column_at - 1) == own_clip)
     right_ok = (column_at < columns * lax.axis_size("wa") - 1) & (clip_of(column_at + 1) == own_clip)
     counts = (
-        edge_count(row_at, rows * lax.axis_size("ha"))[:, None, None, None]
-        * (1.0 + left_ok.astype(jnp.float32) + right_ok.astype(jnp.float32))[None, None, :, None]
-        * edge_count(frame_at, frames * lax.axis_size("ta"))[None, None, None]
+        (1.0 + left_ok.astype(jnp.float32) + right_ok.astype(jnp.float32))[None, :, None]
+        * edge_count(frame_at, frames * lax.axis_size("ta"))[None, None]
     )
-    inverse = jnp.broadcast_to(1.0 / counts, (rows, batch, columns, frames)).reshape(rows, tokens, 1)
+    inverse = jnp.broadcast_to(1.0 / counts, (batch, columns, frames)).reshape(tokens, 1)
     flags = jnp.stack([(ha == 1), (ha == 0)]).astype(jnp.float32)
+    flags = jnp.concatenate([flags, 1.0 / edge_count(row_at, rows * lax.axis_size("ha"))])
     head_bf = head_weight.astype(jnp.bfloat16)
     lag = lambda i: (0, jnp.maximum(i - 2, 0), 0, 0, 0)
     beside = lambda i: (0, jnp.where(i == 0, rows, i - 1), 0, 0)
@@ -290,7 +290,7 @@
             pl.BlockSpec((batch, 1) + ahead.shape[2:], beside),
             pl.BlockSpec((batch, 1, columns, frames, width), lag),
             pl.BlockSpec(pool.shape, whole),
-            pl.BlockSpec((1, tokens, 1), lambda i: (jnp.maximum(i - 2, 0), 0, 0)),
+            pl.BlockSpec((tokens, 1), whole),
             pl.BlockSpec(head_bf.shape, whole),
         ],
         out_specs=[

time: 138 us -> 136 us (0.986)
  local copies, waits for them, and re-layouts: 19.5 us -> 16.8 us
    reshape x1, local copies, waits for them, and re-layouts: 3.91 us -> 1.46 us  [local(): jnp.broadcast_to(1.0 / counts, (batch, columns, frames)).reshape(tokens, 1)]
  transfers between devices with their start and end apart: 6 -> 6, of which waited for: 2 -> 2; matrix products, arithmetic and copies ran while one was open for 19% -> 17% of each run, Pallas kernels for 0% -> 0%
where the time goes in v5:
time: 136 us; the launch traced here: 135 us
  Pallas kernels  86.9 us (64%)
  local copies, waits for them, and re-layouts  16.8 us (12%)
  other arithmetic  12.1 us (9%)
  starting transfers between devices  9.33 us (7%)
  waiting for transfers between devices  7.73 us (6%)
  between operations  2.59 us (2%)
    pallas_call x1, Pallas kernels, local(): pl.pallas_call(functools.partial(fused_kernel, rows), grid=(rows + 2,), i...  44.4 us
    pallas_call x1, Pallas kernels, reduce_and_update(): pl.pallas_call(functools.partial(reduce_kernel, peers), in_specs=[vmem] *...  42.5 us
    reduce_sum x3, other arithmetic, facing_frame(): return jnp.sum(jnp.where(facing, cells, jnp.zeros_like(cells)), axis=-2)  6.87 us
    ppermute x1, waiting for transfers between devices, exchange_halo(): lax.ppermute(column(jnp.minimum(wa + columns - 1, columns - 1)), 'wa', fo...  5.26 us
    ppermute x1, starting transfers between devices, exchange_halo(): lax.ppermute(column(jnp.minimum(wa + columns - 1, columns - 1)), 'wa', fo...  4.92 us
  transfers between devices with their start and end apart: 6, of which 2 were waited for; matrix products, arithmetic and copies ran while one was open for 17% of the time, Pallas kernels for 0%

profile of v5, /device:TPU:0, one launch (start us, length us, event | category | flops | bytes accessed | tf_op | source)
XLA Modules:
  0.0 135.4 jit_solution(3664292610098330791)
XLA Ops:
  0.6 2.0 %dynamic-slice_bitcast_fusion = (bf16[2,14,8,1000]{3,2,1,0:T(8,128)(2,1)}, bf16[2,14,8,1000]{3,2,1,0:T(8,128)(2,1)S(1)}) fusion(bf16[2,8,14,14,1000]{4,1,3,2,0:T(8,128)(2,1)} %param.5, s32[]{:T(128)S(6)} %max.3, s32[]{:T(128)S(6)} %select_n.108), kind=kLoop, calls=%fused_computation.15 | loop fusion | bytes 1792008 | tf_op jit(solution)/shard_map/squeeze | solution.py:41
  2.7 4.9 %collective-permute-start.1 = (bf16[2,14,8,1000]{3,2,1,0:T(8,128)(2,1)S(1)}, bf16[2,14,8,1000]{3,2,1,0:T(8,128)(2,1)S(1)}, u32[]{:S(2)}, u32[]{:S(2)}) collective-permute-start(bf16[2,14,8,1000]{3,2,1,0:T(8,128)(2,1)S(1)} %get-tuple-element.16), channel_id=1, source_target_pairs={{0,1},{1,2},{2,3},{3,4},{4,5},{5,6},{6,7},{8,9},{9,10},{10,11},{11... | collective-permute-start | bytes 1344008 | tf_op jit(solution)/shard_map/ppermute | solution.py:43
  7.6 1.3 collective-permute-start.2
  8.9 1.1 dynamic-slice_bitcast_fusion.2
  9.9 1.6 %collective-permute-start = (bf16[2,1,14,8,1000]{4,3,2,1,0:T(8,128)(2,1)S(1)}, bf16[2,1,14,8,1000]{4,3,2,1,0:T(8,128)(2,1)S(1)}, u32[]{:S(2)}, u32[]{:S(2)}) collective-permute-start(bf16[2,1,14,8,1000]{4,3,2,1,0:T(8,128)(2,1)S(1)} %dynamic-slice_bitcast_fusion.2), channel_id=1, source_target_pairs={{0,8},{8,0},{1,9},{9,1},{2,10},{10,2},{3,11},{11,3},{4,12},{12,4},... | collective-permute-start | bytes 1344008 | tf_op jit(solution)/shard_map/ppermute | solution.py:45
  11.5 0.0 copy-start.2
  11.5 6.0 %select_reduce_fusion = bf16[2,14,14,1000]{3,2,1,0:T(8,128)(2,1)S(1)} fusion(pred[8]{0:T(512)(128)(4,1)S(1)} %iota_compare_fusion, bf16[2,8,14,14,1000]{4,1,3,2,0:T(8,128)(2,1)} %param.5), kind=kLoop, calls=%fused_computation | loop fusion | flops 5880000 | bytes 7056008 | tf_op jit(solution)/shard_map/reduce_sum | solution.py:35
  17.5 1.7 %copy.53 = bf16[2,14,14,1000]{3,0,2,1:T(2,128)(2,1)} copy(bf16[2,14,14,1000]{3,2,1,0:T(8,128)(2,1)S(1)} %select_reduce_fusion) | data formatting | bytes 1568000 | tf_op jit(solution)/shard_map/reduce_sum | solution.py:35
  19.2 0.0 collective-permute-start.4
  19.3 0.0 copy-done.2
  19.4 0.1 concatenate.38
  19.5 0.0 copy-start
  19.5 1.4 %constant_dynamic-slice_fusion = f32[32,1000]{0,1:T(8,128)S(1)} fusion(f32[1024,1000]{0,1:T(8,128)} %param.6, s32[]{:T(128)S(6)} %select_n.122), kind=kLoop, calls=%fused_computation.46 | loop fusion | bytes 256004 | tf_op jit(solution)/shard_map/dynamic_slice | solution.py:315
  20.9 0.1 and_select_fusion.3
  21.0 0.7 fusion.10.pool
  21.7 0.1 multiply_divide_fusion
  21.8 0.1 add_convert_fusion
  21.9 5.3 %collective-permute-done.1 = bf16[2,14,8,1000]{3,2,1,0:T(8,128)(2,1)S(1)} collective-permute-done((bf16[2,14,8,1000]{3,2,1,0:T(8,128)(2,1)S(1)}, bf16[2,14,8,1000]{3,2,1,0:T(8,128)(2,1)S(1)}, u32[]{:S(2)}, u32[]{:S(2)}) %collective-permute-start.1) | collective-permute-done | bytes 448032 | tf_op jit(solution)/shard_map/ppermute | solution.py:43
  27.2 0.0 collective-permute-done.2
  27.2 1.6 %collective-permute-start.3 = (bf16[2,1,16,1000]{3,2,1,0:T(8,128)(2,1)S(1)}, bf16[2,1,16,1000]{3,2,1,0:T(8,128)(2,1)S(1)}, u32[]{:S(2)}, u32[]{:S(2)}) collective-permute-start(bf16[2,1,16,1000]{3,2,1,0:T(8,128)(2,1)S(1)} %constant_dynamic-slice_fusion.1), channel_id=1, source_target_pairs={{0,8},{8,0},{1,9},{9,1},{2,10},{10,2},{3,11},{11,3},{4,12},{12,4},... | collective-permute-start | bytes 192008 | tf_op jit(solution)/shard_map/ppermute | solution.py:48
  28.8 0.0 collective-permute-done.halo_row
  28.8 0.0 copy-start.1
  28.8 0.3 fusion.6
  29.1 2.5 %collective-permute-done.3 = bf16[2,1,16,1000]{3,2,1,0:T(8,128)(2,1)S(1)} collective-permute-done((bf16[2,1,16,1000]{3,2,1,0:T(8,128)(2,1)S(1)}, bf16[2,1,16,1000]{3,2,1,0:T(8,128)(2,1)S(1)}, u32[]{:S(2)}, u32[]{:S(2)}) %collective-permute-start.3) | collective-permute-done | bytes 64032 | tf_op jit(solution)/shard_map/ppermute | solution.py:48
  31.6 0.5 fusion.5
  32.1 0.7 pad_maximum_fusion.2
  32.9 0.0 collective-permute-start.5
  32.9 0.0 copy-done.1
  32.9 0.6 pad_maximum_fusion.3.flags
  33.5 0.0 copy-done
  33.5 0.3 convert_element_type.59
  33.8 0.6 broadcast_in_dim.34
  34.4 1.5 %reshape.191.inverse = f32[224,1]{1,0:T(8,128)} reshape(f32[2,14,8]{2,1,0:T(8,128)} %broadcast_in_dim.34) | data formatting | bytes 1792 | tf_op jit(solution)/shard_map/reshape | solution.py:275
  35.8 2.5 %copy.61.head = bf16[1024,1000]{1,0:T(8,128)(2,1)} copy(bf16[1024,1000]{0,1:T(8,128)(2,1)S(1)} %convert_element_type.59) | data formatting | bytes 4096000 | tf_op jit(solution)/shard_map/convert_element_type | solution.py:278
  38.4 0.8 copy.69.weight
  39.2 1.0 pad_maximum_fusion.sides
  40.3 0.0 collective-permute-done.5
  40.3 1.0 slice_bitcast_fusion.1
  41.3 0.1 copy.57
  41.4 0.1 copy.58
  41.5 0.8 slice_bitcast_fusion.2
  42.3 0.0 collective-permute-done.4
  42.3 1.4 %copy.54 = bf16[2,14,14,1000]{3,2,1,0:T(8,128)(2,1)S(1)} copy(bf16[2,14,14,1000]{3,0,2,1:T(2,128)(2,1)} %collective-permute-done.4) | data formatting | bytes 1568000 | tf_op jit(solution)/shard_map/ppermute | solution.py:46
  43.7 1.5 %pad_maximum_fusion.1.ahead = bf16[2,15,16,1000]{3,2,1,0:T(8,128)(2,1)} fusion(bf16[2,15,1,1000]{3,2,1,0:T(2,128)(2,1)S(1)} %copy.58, bf16[2,15,1,1000]{3,2,1,0:T(2,128)(2,1)S(1)} %copy.57, bf16[2,1,14,1000]{3,2,1,0:T(8,128)(2,1)S(1)} %slice_bitcast_fusion.2, bf16[2,14,14,1000]{3,2,1,0:T(8,128)(2,1)S(1)} %copy.54), kind=kLoop, calls=%fused_computation.4 | loop fusion | flops 3840000 | bytes 1920000 | tf_op jit(solution)/shard_map/concatenate | solution.py:55
  45.2 44.4 %shard_map.67 = (bf16[2,14,14,8,1024]{4,3,2,1,0:T(8,128)(2,1)}, bf16[1024,1000]{1,0:T(8,128)(2,1)}, f32[1,1]{1,0:T(1,128)}) custom-call(f32[16]{0:T(128)} %pad_maximum_fusion.3.flags, bf16[2,14,14,8,1000]{4,3,2,1,0:T(8,128)(2,1)} %bitcast.32, bf16[2,1,14,8,1000]{4,3,2,1,0:T(8,128)(2,1)} %copy-done.1, bf16[2,15,16,1000]{3,2,1,0:T(8,128)(2,1)} %pad_maximum_fusion.sides, ...), custom_call_target="tpu_custom_call" | custom-call | tf_op jit(solution)/shard_map/pallas_call | solution.py:282
  89.6 42.5 %shard_map.68 = (f32[32,1000]{1,0:T(8,128)}, f32[1,1]{1,0:T(1,128)}) custom-call(bf16[2,16,32,1000]{3,2,1,0:T(8,128)(2,1)} %bitcast.34, f32[1,1]{1,0:T(1,128)} %get-tuple-element.10.local_loss, f32[32,1000]{1,0:T(8,128)} %copy.69.weight), custom_call_target="tpu_custom_call" | custom-call | tf_op jit(solution)/shard_map/pallas_call | solution.py:235
  132.7 1.6 %copy.75 = f32[32,1000]{1,0:T(8,128)} copy(f32[32,1000]{1,0:T(8,128)} %get-tuple-element.26) | data formatting | bytes 256000
  (16 shorter events, 0.2 us)
Async XLA Ops:
  2.7 24.5 %collective-permute-start.1 = (bf16[2,14,8,1000]{3,2,1,0:T(8,128)(2,1)S(1)}, bf16[2,14,8,1000]{3,2,1,0:T(8,128)(2,1)S(1)}, u32[]{:S(2)}, u32[]{:S(2)}) collective-permute-start(bf16[2,14,8,1000]{3,2,1,0:T(8,128)(2,1)S(1)} %get-tuple-element.16), channel_id=1, source_target_pairs={{0,1},{1,2},{2,3},{3,4},{4,5},{5,6},{6,7},{8,9},{9,10},{10,11},{11... | collective-permute-start | bytes 1344008 | tf_op jit(solution)/shard_map/ppermute | solution.py:43
  7.6 19.6 %collective-permute-start.2 = (bf16[2,14,8,1000]{3,2,1,0:T(8,128)(2,1)}, bf16[2,14,8,1000]{3,2,1,0:T(8,128)(2,1)S(1)}, u32[]{:S(2)}, u32[]{:S(2)}) collective-permute-start(bf16[2,14,8,1000]{3,2,1,0:T(8,128)(2,1)} %get-tuple-element.15), channel_id=1, source_target_pairs={{1,0},{2,1},{3,2},{4,3},{5,4},{6,5},{7,6},{9,8},{10,9},{11,10},{12... | collective-permute-start | bytes 1344008 | tf_op jit(solution)/shard_map/ppermute | solution.py:44
  9.9 18.9 %collective-permute-start = (bf16[2,1,14,8,1000]{4,3,2,1,0:T(8,128)(2,1)S(1)}, bf16[2,1,14,8,1000]{4,3,2,1,0:T(8,128)(2,1)S(1)}, u32[]{:S(2)}, u32[]{:S(2)}) collective-permute-start(bf16[2,1,14,8,1000]{4,3,2,1,0:T(8,128)(2,1)S(1)} %dynamic-slice_bitcast_fusion.2), channel_id=1, source_target_pairs={{0,8},{8,0},{1,9},{9,1},{2,10},{10,2},{3,11},{11,3},{4,12},{12,4},... | collective-permute-start | bytes 1344008 | tf_op jit(solution)/shard_map/ppermute | solution.py:45
  11.5 7.8 %copy-start.2 = (s32[2]{0:T(128)S(1)}, s32[2]{0:T(128)}, u32[]{:S(2)}) copy-start(s32[2]{0:T(128)} %constant.145.clone) | copy-start | bytes 28
  19.2 23.1 %collective-permute-start.4 = (bf16[2,14,14,1000]{3,0,2,1:T(2,128)(2,1)}, bf16[2,14,14,1000]{3,0,2,1:T(2,128)(2,1)}, u32[]{:S(2)}, u32[]{:S(2)}) collective-permute-start(bf16[2,14,14,1000]{3,0,2,1:T(2,128)(2,1)} %copy.53), channel_id=1, source_target_pairs={{0,16},{16,0},{1,17},{17,1},{2,18},{18,2},{3,19},{19,3},{4,20},{20... | collective-permute-start | bytes 2352008 | tf_op jit(solution)/shard_map/ppermute | solution.py:46
  19.5 14.0 %copy-start = (f32[1024,1000]{0,1:T(8,128)S(1)}, f32[1024,1000]{0,1:T(8,128)}, u32[]{:S(2)}) copy-start(f32[1024,1000]{0,1:T(8,128)} %param.6) | copy-start | bytes 12288004
  27.2 4.3 %collective-permute-start.3 = (bf16[2,1,16,1000]{3,2,1,0:T(8,128)(2,1)S(1)}, bf16[2,1,16,1000]{3,2,1,0:T(8,128)(2,1)S(1)}, u32[]{:S(2)}, u32[]{:S(2)}) collective-permute-start(bf16[2,1,16,1000]{3,2,1,0:T(8,128)(2,1)S(1)} %constant_dynamic-slice_fusion.1), channel_id=1, source_target_pairs={{0,8},{8,0},{1,9},{9,1},{2,10},{10,2},{3,11},{11,3},{4,12},{12,4},... | collective-permute-start | bytes 192008 | tf_op jit(solution)/shard_map/ppermute | solution.py:48
  28.8 4.1 %copy-start.1 = (bf16[2,1,14,8,1000]{4,3,2,1,0:T(8,128)(2,1)}, bf16[2,1,14,8,1000]{4,3,2,1,0:T(8,128)(2,1)S(1)}, u32[]{:S(2)}) copy-start(bf16[2,1,14,8,1000]{4,3,2,1,0:T(8,128)(2,1)S(1)} %collective-permute-done.halo_row) | copy-start | bytes 1344004
  32.9 7.4 %collective-permute-start.5 = (bf16[2,44,1000]{2,1,0:T(8,128)(2,1)}, bf16[2,44,1000]{2,1,0:T(8,128)(2,1)}, u32[]{:S(2)}, u32[]{:S(2)}) collective-permute-start(bf16[2,44,1000]{2,1,0:T(8,128)(2,1)} %pad_maximum_fusion.2), channel_id=1, source_target_pairs={{0,16},{16,0},{1,17},{17,1},{2,18},{18,2},{3,19},{19,3},{4,20},{20... | collective-permute-start | bytes 528008 | tf_op jit(solution)/shard_map/ppermute | solution.py:51
